TPU v7x, 256 devices: a whole 4x4x8 slice. The times are simulated.
256 devices in a mesh: dom: 64 (over z, y, core), chan: 4 (over x).
Axes of the slice: x: 4, y: 4, z: 8, core: 2. Of those that a mesh axis runs over, the one named last changes fastest.
Arguments:
- features: bfloat16 [256, 65536], P('chan', 'dom'), may hold values from -6 to 6
- cotangent: bfloat16 [256, 65536], P('chan', 'dom'), may hold values from -6 to 6
- weights: bfloat16 [9, 256, 256], P(None, 'chan'), may hold values from -0.375 to 0.375
- tile_values: float32 [4096, 128, 128], P('dom'), may hold values from -0.046875 to 0.046875
- tile_cols: int32 [64, 8, 8], P('dom'), may hold values from 0 to 11, as said below
- send_list: int32 [64, 4, 128], P('dom'), may hold values from 0 to 1023
Outputs:
- input_grad: float32 [256, 65536], P('chan', 'dom')
- weight_grad: float32 [9, 256, 256], P(None, None, 'chan')
Inputs may be any that keep to these rules, and one draw needn't show every extreme that they name: `tile_cols`: values below 8 are blocks of the partition's own nodes; 8 + s is the block received from neighbour slot s. Tile 0 of row block r has column block r.
All inputs are finite; a program needn't handle non-finite values.
Results may differ from a plain program's by a relative error of at most 0.0003.
Values may be sent and summed in bfloat16 or wider, within the bound.
A program may use at most 128 MiB of HBM per device.

v0:
```python
import jax
import jax.numpy as jnp
from jax import lax
from jax.sharding import PartitionSpec as P

NEIGHBOUR_SHIFTS = (1, -1, 2, -2)


def from_behind(block, axis, distance):
    devices = range(lax.axis_size(axis))
    route = [((i - distance) % len(devices), i) for i in devices]
    return lax.ppermute(block, axis, route)


def exchange_rows(outgoing):
    received = [
        from_behind(outgoing[:, slot_index], "dom", offset)
        for slot_index, offset in enumerate(NEIGHBOUR_SHIFTS)
    ]
    return received


def apply_operator(field_in, tile_values, tile_cols, send_list):
    channels, local_nodes = field_in.shape
    tile_size = tile_values.shape[-1]
    per_row = tile_cols.shape[-1]
    outgoing = jnp.take(field_in, send_list[0], axis=1)
    received = exchange_rows(outgoing)
    extended = jnp.concatenate([field_in] + received, axis=1)
    blocks = extended.reshape(channels, -1, tile_size)
    picked = jnp.take(blocks, tile_cols.reshape(-1), axis=1)
    product = jnp.einsum("ctj,tjk->ctk", picked, tile_values, precision=lax.Precision.HIGHEST)
    return (
        product.reshape(channels, -1, per_row, tile_size).sum(axis=2).reshape(channels, local_nodes)
    )


def local(features, cotangent, weights, tile_values, tile_cols, send_list):
    top_order = weights.shape[0] - 1
    local_nodes = features.shape[1]

    def operator_on(field_in):
        return apply_operator(field_in, tile_values, tile_cols, send_list)

    feat_all, cot_all = (
        lax.all_gather(features, "chan", axis=0, tiled=True),
        lax.all_gather(cotangent, "chan", axis=0, tiled=True),
    )
    feat_wide = feat_all.astype(jnp.float32)

    def mixed_term(order_index):
        return jnp.dot(weights[order_index], cot_all, preferred_element_type=jnp.float32)

    def grad_term(state):
        return lax.dot_general(
            feat_wide, state, (((1,), (1,)), ((), ())), precision=lax.Precision.HIGHEST
        )

    cheb_prev = cotangent.astype(jnp.float32)
    grad_terms = [grad_term(cheb_prev)]
    cheb_now = operator_on(cheb_prev)
    grad_terms.append(grad_term(cheb_now))
    for order_index in range(2, top_order + 1):
        cheb_prev, cheb_now = (cheb_now, 2.0 * operator_on(cheb_now) - cheb_prev)
        grad_terms.append(grad_term(cheb_now))
    current = mixed_term(top_order)
    clen_later = jnp.zeros_like(current)
    for order_index in range(top_order - 1, 0, -1):
        current, clen_later = (
            mixed_term(order_index) + 2.0 * operator_on(current) - clen_later,
            current,
        )
    input_grad = mixed_term(0) + operator_on(current) - clen_later
    local_grads = jnp.stack(grad_terms)
    summed = lax.psum(local_grads, "dom")
    nodes_all = lax.axis_size("dom") * local_nodes
    return (input_grad, summed * float(nodes_all) ** (-0.5))


def solution(mesh):
    placed = (
        P("chan", "dom"),
        P("chan", "dom"),
        P(None, "chan", None),
        P("dom", None, None),
        P("dom", None, None),
        P("dom", None, None),
    )
    return jax.shard_map(
        local,
        mesh=mesh,
        in_specs=placed,
        out_specs=(P("chan", "dom"), P(None, None, "chan")),
        check_vma=False,
    )
```

profile of v0, /device:TPU:2, one launch (start us, length us, event | category | flops | bytes accessed | tf_op | source)
XLA Modules:
  0.0 664.3 jit_solution(9862079954037837758)
XLA Ops:
  8.6 13.7 %all_gather.6 = bf16[256,1024]{1,0:T(8,128)(2,1)S(1)} all-gather(bf16[64,1024]{1,0:T(8,128)(2,1)} %param.11), channel_id=1, replica_groups=mesh['dom'=64,'chan'=4] {'chan'}, dimensions={0}, use_global_device_ids=true | all-gather | bytes 655360 | tf_op jit(solution)/shard_map/all_gather | solution.py:47
  26.1 5.1 collective-permute-start.1
  31.2 5.3 collective-permute-start.3
  38.1 12.8 %all_gather.7 = bf16[256,1024]{1,0:T(8,128)(2,1)S(1)} all-gather(bf16[64,1024]{1,0:T(8,128)(2,1)S(1)} %copy-done.13), channel_id=1, replica_groups=mesh['dom'=64,'chan'=4] {'chan'}, dimensions={0}, use_global_device_ids=true | all-gather | bytes 655360 | tf_op jit(solution)/shard_map/all_gather | solution.py:46
  51.8 3.5 collective-permute-start.33
  57.3 7.7 %collective-permute-done.34 = f32[64,128]{0,1:T(8,128)S(1)} collective-permute-done((f32[64,128]{0,1:T(8,128)S(1)}, f32[64,128]{0,1:T(8,128)S(1)}, u32[]{:S(2)}, u32[]{:S(2)}) %collective-permute-start.34) | collective-permute-done | bytes 32800 | tf_op jit(solution)/shard_map/ppermute | solution.py:12
  65.2 4.2 collective-permute-done.35
  70.4 6.4 bitcast_reduce_fusion.7
  86.4 2.0 gather_fusion.1
  88.4 6.7 %bitcast_reduce_fusion.15 = f32[64,8,128]{2,0,1:T(8,128)S(1)} fusion(f32[64,128,128]{2,1,0:T(8,128)} %param.13, f32[64,64,128]{2,1,0:T(8,128)} %gather_fusion.1, pred[64]{0:T(512)(128)(4,1)S(1)} %compare_and_fusion), kind=kOutput, calls=%fused_computation.47 | convolution fusion | flops 806289408 | bytes 6553664 | tf_op jit(solution)/shard_map/ctj,tjk->ctk/dot_general | solution.py:32
  97.6 5.1 collective-permute-start.5
  102.7 5.3 collective-permute-start.7
  110.1 5.5 collective-permute-start.37
  115.6 5.3 collective-permute-start.39
  121.0 2.0 gather_fusion.3
  123.1 6.7 %bitcast_reduce_fusion.14 = f32[64,8,128]{2,0,1:T(8,128)S(1)} fusion(f32[64,128,128]{2,1,0:T(8,128)} %param.13, f32[64,64,128]{2,1,0:T(8,128)} %gather_fusion.3, pred[64]{0:T(512)(128)(4,1)S(1)} %compare_and_fusion), kind=kOutput, calls=%fused_computation.46 | convolution fusion | flops 806289408 | bytes 6553664 | tf_op jit(solution)/shard_map/ctj,tjk->ctk/dot_general | solution.py:32
  132.8 5.1 collective-permute-start.9
  140.8 5.5 collective-permute-start.11
  150.6 2.0 gather_fusion.19
  152.7 6.7 %bitcast_reduce_fusion.6 = f32[64,8,128]{2,0,1:T(8,128)S(1)} fusion(f32[64,128,128]{2,1,0:T(8,128)} %param.13, f32[64,64,128]{2,1,0:T(8,128)} %gather_fusion.19, pred[64]{0:T(512)(128)(4,1)S(1)} %compare_and_fusion), kind=kOutput, calls=%fused_computation.38 | convolution fusion | flops 806289408 | bytes 6553664 | tf_op jit(solution)/shard_map/ctj,tjk->ctk/dot_general | solution.py:32
  167.0 5.1 collective-permute-start.41
  172.1 5.5 collective-permute-start.43
  177.7 2.0 gather_fusion.5
  179.7 6.7 %bitcast_reduce_fusion.13 = f32[64,8,128]{2,0,1:T(8,128)S(1)} fusion(f32[64,128,128]{2,1,0:T(8,128)} %param.13, f32[64,64,128]{2,1,0:T(8,128)} %gather_fusion.5, pred[64]{0:T(512)(128)(4,1)S(1)} %compare_and_fusion), kind=kOutput, calls=%fused_computation.45 | convolution fusion | flops 806289408 | bytes 6553664 | tf_op jit(solution)/shard_map/ctj,tjk->ctk/dot_general | solution.py:32
  190.1 5.1 collective-permute-start.13
  198.1 5.6 collective-permute-start.15
  208.0 2.0 gather_fusion.21
  210.0 6.7 %bitcast_reduce_fusion.5 = f32[64,8,128]{2,0,1:T(8,128)S(1)} fusion(f32[64,128,128]{2,1,0:T(8,128)} %param.13, f32[64,64,128]{2,1,0:T(8,128)} %gather_fusion.21, pred[64]{0:T(512)(128)(4,1)S(1)} %compare_and_fusion), kind=kOutput, calls=%fused_computation.37 | convolution fusion | flops 806289408 | bytes 6553664 | tf_op jit(solution)/shard_map/ctj,tjk->ctk/dot_general | solution.py:32
  222.8 5.1 collective-permute-start.45
  230.5 5.8 collective-permute-start.47
  240.1 2.0 gather_fusion.7
  242.1 6.7 %bitcast_reduce_fusion.12 = f32[64,8,128]{2,0,1:T(8,128)S(1)} fusion(f32[64,128,128]{2,1,0:T(8,128)} %param.13, f32[64,64,128]{2,1,0:T(8,128)} %gather_fusion.7, pred[64]{0:T(512)(128)(4,1)S(1)} %compare_and_fusion), kind=kOutput, calls=%fused_computation.44 | convolution fusion | flops 806289408 | bytes 6553664 | tf_op jit(solution)/shard_map/ctj,tjk->ctk/dot_general | solution.py:32
  252.6 5.1 collective-permute-start.17
  259.7 5.5 collective-permute-start.19
  268.7 2.0 gather_fusion.23
  270.7 6.7 %bitcast_reduce_fusion.4 = f32[64,8,128]{2,0,1:T(8,128)S(1)} fusion(f32[64,128,128]{2,1,0:T(8,128)} %param.13, f32[64,64,128]{2,1,0:T(8,128)} %gather_fusion.23, pred[64]{0:T(512)(128)(4,1)S(1)} %compare_and_fusion), kind=kOutput, calls=%fused_computation.36 | convolution fusion | flops 806289408 | bytes 6553664 | tf_op jit(solution)/shard_map/ctj,tjk->ctk/dot_general | solution.py:32
  281.7 5.1 collective-permute-start.49
  288.3 5.5 collective-permute-start.51
  295.4 2.0 gather_fusion.9
  297.4 6.7 %bitcast_reduce_fusion.11 = f32[64,8,128]{2,0,1:T(8,128)S(1)} fusion(f32[64,128,128]{2,1,0:T(8,128)} %param.13, f32[64,64,128]{2,1,0:T(8,128)} %gather_fusion.9, pred[64]{0:T(512)(128)(4,1)S(1)} %compare_and_fusion), kind=kOutput, calls=%fused_computation.43 | convolution fusion | flops 806289408 | bytes 6553664 | tf_op jit(solution)/shard_map/ctj,tjk->ctk/dot_general | solution.py:32
  307.3 5.0 collective-permute-start.21
  314.4 5.6 collective-permute-start.23
  323.5 2.0 gather_fusion.25
  325.5 6.7 %bitcast_reduce_fusion.3 = f32[64,8,128]{2,0,1:T(8,128)S(1)} fusion(f32[64,128,128]{2,1,0:T(8,128)} %param.13, f32[64,64,128]{2,1,0:T(8,128)} %gather_fusion.25, pred[64]{0:T(512)(128)(4,1)S(1)} %compare_and_fusion), kind=kOutput, calls=%fused_computation.35 | convolution fusion | flops 806289408 | bytes 6553664 | tf_op jit(solution)/shard_map/ctj,tjk->ctk/dot_general | solution.py:32
  336.4 5.1 collective-permute-start.53
  341.6 5.8 collective-permute-start.55
  347.4 2.0 gather_fusion.11
  349.5 6.7 %bitcast_reduce_fusion.10 = f32[64,8,128]{2,0,1:T(8,128)S(1)} fusion(f32[64,128,128]{2,1,0:T(8,128)} %param.13, f32[64,64,128]{2,1,0:T(8,128)} %gather_fusion.11, pred[64]{0:T(512)(128)(4,1)S(1)} %compare_and_fusion), kind=kOutput, calls=%fused_computation.42 | convolution fusion | flops 806289408 | bytes 6553664 | tf_op jit(solution)/shard_map/ctj,tjk->ctk/dot_general | solution.py:32
  359.9 5.1 collective-permute-start.25
  367.1 5.5 collective-permute-start.27
  376.1 2.0 gather_fusion.27
  378.1 6.7 %bitcast_reduce_fusion.2 = f32[64,8,128]{2,0,1:T(8,128)S(1)} fusion(f32[64,128,128]{2,1,0:T(8,128)} %param.13, f32[64,64,128]{2,1,0:T(8,128)} %gather_fusion.27, pred[64]{0:T(512)(128)(4,1)S(1)} %compare_and_fusion), kind=kOutput, calls=%fused_computation.34 | convolution fusion | flops 806289408 | bytes 6553664 | tf_op jit(solution)/shard_map/ctj,tjk->ctk/dot_general | solution.py:32
  389.0 5.1 collective-permute-start.57
  395.6 5.5 collective-permute-start.59
  404.7 6.7 %bitcast_reduce_fusion.9 = f32[64,8,128]{2,0,1:T(8,128)S(1)} fusion(f32[64,128,128]{2,1,0:T(8,128)} %param.13, f32[64,64,128]{2,1,0:T(8,128)} %gather_fusion.13, pred[64]{0:T(512)(128)(4,1)S(1)} %compare_and_fusion), kind=kOutput, calls=%fused_computation.41 | convolution fusion | flops 806289408 | bytes 6553664 | tf_op jit(solution)/shard_map/ctj,tjk->ctk/dot_general | solution.py:32
  415.2 5.1 collective-permute-start.29
  422.4 5.6 collective-permute-start.31
  433.5 6.7 %bitcast_reduce_fusion.1 = f32[64,8,128]{2,0,1:T(8,128)S(1)} fusion(f32[64,128,128]{2,1,0:T(8,128)} %param.13, f32[64,64,128]{2,1,0:T(8,128)} %gather_fusion.29, pred[64]{0:T(512)(128)(4,1)S(1)} %compare_and_fusion), kind=kOutput, calls=%fused_computation.33 | convolution fusion | flops 806289408 | bytes 6553664 | tf_op jit(solution)/shard_map/ctj,tjk->ctk/dot_general | solution.py:32
  443.8 5.0 collective-permute-start.61
  450.4 5.6 collective-permute-start.63
  463.5 2.1 gather_fusion.31
  465.5 6.7 %bitcast_reduce_fusion = f32[64,8,128]{2,0,1:T(8,128)S(1)} fusion(f32[64,128,128]{2,1,0:T(8,128)} %param.13, f32[64,64,128]{2,1,0:T(8,128)} %gather_fusion.31, pred[64]{0:T(512)(128)(4,1)S(1)} %compare_and_fusion), kind=kOutput, calls=%fused_computation.32 | convolution fusion | flops 806289408 | bytes 6553664 | tf_op jit(solution)/shard_map/ctj,tjk->ctk/dot_general | solution.py:32
  473.8 6.7 %bitcast_reduce_fusion.8 = f32[64,8,128]{2,0,1:T(8,128)S(1)} fusion(f32[64,128,128]{2,1,0:T(8,128)} %param.13, f32[64,64,128]{2,1,0:T(8,128)} %gather_fusion.15, pred[64]{0:T(512)(128)(4,1)S(1)} %compare_and_fusion), kind=kOutput, calls=%fused_computation.40 | convolution fusion | flops 806289408 | bytes 6553664 | tf_op jit(solution)/shard_map/ctj,tjk->ctk/dot_general | solution.py:32
  482.2 172.9 %all-reduce.2.cloned.1.call-done = f32[9,256,64]{1,2,0:T(8,128)} async-done(((f32[9,256,64]{1,2,0:T(8,128)}), f32[9,256,64]{1,2,0:T(8,128)}) %all-reduce.2.cloned.1.call-update) | async-done | bytes 589840 | tf_op jit(solution)/shard_map/psum | solution.py:75
  (328 shorter events, 143.2 us)
Async XLA Ops:
  7.2 647.9 %all-reduce.2.cloned.1.call-start = ((), (), s32[]{:S(2)}) async-start(), calls=%async_computation | async-start | bytes 1179648 | tf_op jit(solution)/shard_map/psum | solution.py:75
  26.1 52.7 %collective-permute-start = (f32[64,128]{1,0:T(8,128)}, f32[64,128]{1,0:T(8,128)}, u32[]{:S(2)}, u32[]{:S(2)}) collective-permute-start(f32[64,128]{1,0:T(8,128)} %get-tuple-element.67), channel_id=1, source_target_pairs={{252,0},{0,4},{4,8},{8,12},{12,16},{16,20},{20,24},{24,28},{28,32}... | collective-permute-start | bytes 98312 | tf_op jit(solution)/shard_map/ppermute | solution.py:12
  26.1 54.0 %collective-permute-start.1 = (f32[64,128]{1,0:T(8,128)}, f32[64,128]{1,0:T(8,128)}, u32[]{:S(2)}, u32[]{:S(2)}) collective-permute-start(f32[64,128]{1,0:T(8,128)} %get-tuple-element.66), channel_id=1, source_target_pairs={{4,0},{8,4},{12,8},{16,12},{20,16},{24,20},{28,24},{32,28},{36,32}... | collective-permute-start | bytes 98312 | tf_op jit(solution)/shard_map/ppermute | solution.py:12
  31.2 50.4 %collective-permute-start.2 = (f32[64,128]{1,0:T(8,128)}, f32[64,128]{1,0:T(8,128)}, u32[]{:S(2)}, u32[]{:S(2)}) collective-permute-start(f32[64,128]{1,0:T(8,128)} %get-tuple-element.65), channel_id=1, source_target_pairs={{248,0},{252,4},{0,8},{4,12},{8,16},{12,20},{16,24},{20,28},{24,32... | collective-permute-start | bytes 98312 | tf_op jit(solution)/shard_map/ppermute | solution.py:12
  31.2 52.8 %collective-permute-start.3 = (f32[64,128]{1,0:T(8,128)}, f32[64,128]{1,0:T(8,128)}, u32[]{:S(2)}, u32[]{:S(2)}) collective-permute-start(f32[64,128]{1,0:T(8,128)} %get-tuple-element.64), channel_id=1, source_target_pairs={{8,0},{12,4},{16,8},{20,12},{24,16},{28,20},{32,24},{36,28},{40,32... | collective-permute-start | bytes 98312 | tf_op jit(solution)/shard_map/ppermute | solution.py:12
  38.0 13.9 %collective-permute-start.32 = (f32[64,128]{0,1:T(8,128)S(1)}, f32[64,128]{0,1:T(8,128)S(1)}, u32[]{:S(2)}, u32[]{:S(2)}) collective-permute-start(f32[64,128]{0,1:T(8,128)S(1)} %get-tuple-element.35), channel_id=1, source_target_pairs={{252,0},{0,4},{4,8},{8,12},{12,16},{16,20},{20,24},{24,28},{28,32}... | collective-permute-start | bytes 98312 | tf_op jit(solution)/shard_map/ppermute | solution.py:12
  51.8 5.4 collective-permute-start.33
  57.3 7.8 %collective-permute-start.34 = (f32[64,128]{0,1:T(8,128)S(1)}, f32[64,128]{0,1:T(8,128)S(1)}, u32[]{:S(2)}, u32[]{:S(2)}) collective-permute-start(f32[64,128]{0,1:T(8,128)S(1)} %get-tuple-element.33), channel_id=1, source_target_pairs={{248,0},{252,4},{0,8},{4,12},{8,16},{12,20},{16,24},{20,28},{24,32... | collective-permute-start | bytes 98312 | tf_op jit(solution)/shard_map/ppermute | solution.py:12
  97.5 12.6 %collective-permute-start.4 = (f32[64,128]{1,0:T(8,128)S(1)}, f32[64,128]{1,0:T(8,128)S(1)}, u32[]{:S(2)}, u32[]{:S(2)}) collective-permute-start(f32[64,128]{1,0:T(8,128)S(1)} %get-tuple-element.63), channel_id=1, source_target_pairs={{252,0},{0,4},{4,8},{8,12},{12,16},{16,20},{20,24},{24,28},{28,32}... | collective-permute-start | bytes 98312 | tf_op jit(solution)/shard_map/ppermute | solution.py:12
  97.6 18.0 %collective-permute-start.5 = (f32[64,128]{1,0:T(8,128)S(1)}, f32[64,128]{1,0:T(8,128)S(1)}, u32[]{:S(2)}, u32[]{:S(2)}) collective-permute-start(f32[64,128]{1,0:T(8,128)S(1)} %get-tuple-element.62), channel_id=1, source_target_pairs={{4,0},{8,4},{12,8},{16,12},{20,16},{24,20},{28,24},{32,28},{36,32}... | collective-permute-start | bytes 98312 | tf_op jit(solution)/shard_map/ppermute | solution.py:12
  102.7 13.0 %collective-permute-start.6 = (f32[64,128]{1,0:T(8,128)S(1)}, f32[64,128]{1,0:T(8,128)S(1)}, u32[]{:S(2)}, u32[]{:S(2)}) collective-permute-start(f32[64,128]{1,0:T(8,128)S(1)} %get-tuple-element.61), channel_id=1, source_target_pairs={{248,0},{252,4},{0,8},{4,12},{8,16},{12,20},{16,24},{20,28},{24,32... | collective-permute-start | bytes 98312 | tf_op jit(solution)/shard_map/ppermute | solution.py:12
  102.7 18.3 %collective-permute-start.7 = (f32[64,128]{1,0:T(8,128)S(1)}, f32[64,128]{1,0:T(8,128)S(1)}, u32[]{:S(2)}, u32[]{:S(2)}) collective-permute-start(f32[64,128]{1,0:T(8,128)S(1)} %get-tuple-element.60), channel_id=1, source_target_pairs={{8,0},{12,4},{16,8},{20,12},{24,16},{28,20},{32,24},{36,28},{40,32... | collective-permute-start | bytes 98312 | tf_op jit(solution)/shard_map/ppermute | solution.py:12
  110.1 22.7 %collective-permute-start.36 = (f32[64,128]{0,1:T(8,128)}, f32[64,128]{0,1:T(8,128)}, u32[]{:S(2)}, u32[]{:S(2)}) collective-permute-start(f32[64,128]{0,1:T(8,128)} %get-tuple-element.31), channel_id=1, source_target_pairs={{252,0},{0,4},{4,8},{8,12},{12,16},{16,20},{20,24},{24,28},{28,32}... | collective-permute-start | bytes 98312 | tf_op jit(solution)/shard_map/ppermute | solution.py:12
  110.1 29.3 %collective-permute-start.37 = (f32[64,128]{0,1:T(8,128)}, f32[64,128]{0,1:T(8,128)}, u32[]{:S(2)}, u32[]{:S(2)}) collective-permute-start(f32[64,128]{0,1:T(8,128)} %get-tuple-element.30), channel_id=1, source_target_pairs={{4,0},{8,4},{12,8},{16,12},{20,16},{24,20},{28,24},{32,28},{36,32}... | collective-permute-start | bytes 98312 | tf_op jit(solution)/shard_map/ppermute | solution.py:12
  115.6 25.2 %collective-permute-start.38 = (f32[64,128]{0,1:T(8,128)}, f32[64,128]{0,1:T(8,128)}, u32[]{:S(2)}, u32[]{:S(2)}) collective-permute-start(f32[64,128]{0,1:T(8,128)} %get-tuple-element.29), channel_id=1, source_target_pairs={{248,0},{252,4},{0,8},{4,12},{8,16},{12,20},{16,24},{20,28},{24,32... | collective-permute-start | bytes 98312 | tf_op jit(solution)/shard_map/ppermute | solution.py:12
  115.6 32.1 %collective-permute-start.39 = (f32[64,128]{0,1:T(8,128)}, f32[64,128]{0,1:T(8,128)}, u32[]{:S(2)}, u32[]{:S(2)}) collective-permute-start(f32[64,128]{0,1:T(8,128)} %get-tuple-element.28), channel_id=1, source_target_pairs={{8,0},{12,4},{16,8},{20,12},{24,16},{28,20},{32,24},{36,28},{40,32... | collective-permute-start | bytes 98312 | tf_op jit(solution)/shard_map/ppermute | solution.py:12
  132.8 34.2 %collective-permute-start.8 = (f32[64,128]{1,0:T(8,128)}, f32[64,128]{1,0:T(8,128)S(1)}, u32[]{:S(2)}, u32[]{:S(2)}) collective-permute-start(f32[64,128]{1,0:T(8,128)} %get-tuple-element.59), channel_id=1, source_target_pairs={{252,0},{0,4},{4,8},{8,12},{12,16},{16,20},{20,24},{24,28},{28,32}... | collective-permute-start | bytes 98312 | tf_op jit(solution)/shard_map/ppermute | solution.py:12
  132.8 39.2 %collective-permute-start.9 = (f32[64,128]{1,0:T(8,128)}, f32[64,128]{1,0:T(8,128)S(1)}, u32[]{:S(2)}, u32[]{:S(2)}) collective-permute-start(f32[64,128]{1,0:T(8,128)} %get-tuple-element.58), channel_id=1, source_target_pairs={{4,0},{8,4},{12,8},{16,12},{20,16},{24,20},{28,24},{32,28},{36,32}... | collective-permute-start | bytes 98312 | tf_op jit(solution)/shard_map/ppermute | solution.py:12
  139.3 32.7 %collective-permute-start.10 = (f32[64,128]{1,0:T(8,128)}, f32[64,128]{1,0:T(8,128)S(1)}, u32[]{:S(2)}, u32[]{:S(2)}) collective-permute-start(f32[64,128]{1,0:T(8,128)} %get-tuple-element.57), channel_id=1, source_target_pairs={{248,0},{252,4},{0,8},{4,12},{8,16},{12,20},{16,24},{20,28},{24,32... | collective-permute-start | bytes 98312 | tf_op jit(solution)/shard_map/ppermute | solution.py:12
  140.8 36.8 %collective-permute-start.11 = (f32[64,128]{1,0:T(8,128)}, f32[64,128]{1,0:T(8,128)S(1)}, u32[]{:S(2)}, u32[]{:S(2)}) collective-permute-start(f32[64,128]{1,0:T(8,128)} %get-tuple-element.56), channel_id=1, source_target_pairs={{8,0},{12,4},{16,8},{20,12},{24,16},{28,20},{32,24},{36,28},{40,32... | collective-permute-start | bytes 98312 | tf_op jit(solution)/shard_map/ppermute | solution.py:12
  167.0 23.1 %collective-permute-start.40 = (f32[64,128]{0,1:T(8,128)}, f32[64,128]{0,1:T(8,128)}, u32[]{:S(2)}, u32[]{:S(2)}) collective-permute-start(f32[64,128]{0,1:T(8,128)} %get-tuple-element.27), channel_id=1, source_target_pairs={{252,0},{0,4},{4,8},{8,12},{12,16},{16,20},{20,24},{24,28},{28,32}... | collective-permute-start | bytes 98312 | tf_op jit(solution)/shard_map/ppermute | solution.py:12
  167.0 29.6 %collective-permute-start.41 = (f32[64,128]{0,1:T(8,128)}, f32[64,128]{0,1:T(8,128)}, u32[]{:S(2)}, u32[]{:S(2)}) collective-permute-start(f32[64,128]{0,1:T(8,128)} %get-tuple-element.26), channel_id=1, source_target_pairs={{4,0},{8,4},{12,8},{16,12},{20,16},{24,20},{28,24},{32,28},{36,32}... | collective-permute-start | bytes 98312 | tf_op jit(solution)/shard_map/ppermute | solution.py:12
  172.1 26.0 %collective-permute-start.42 = (f32[64,128]{0,1:T(8,128)}, f32[64,128]{0,1:T(8,128)}, u32[]{:S(2)}, u32[]{:S(2)}) collective-permute-start(f32[64,128]{0,1:T(8,128)} %get-tuple-element.25), channel_id=1, source_target_pairs={{248,0},{252,4},{0,8},{4,12},{8,16},{12,20},{16,24},{20,28},{24,32... | collective-permute-start | bytes 98312 | tf_op jit(solution)/shard_map/ppermute | solution.py:12
  172.1 33.0 %collective-permute-start.43 = (f32[64,128]{0,1:T(8,128)}, f32[64,128]{0,1:T(8,128)}, u32[]{:S(2)}, u32[]{:S(2)}) collective-permute-start(f32[64,128]{0,1:T(8,128)} %get-tuple-element.24), channel_id=1, source_target_pairs={{8,0},{12,4},{16,8},{20,12},{24,16},{28,20},{32,24},{36,28},{40,32... | collective-permute-start | bytes 98312 | tf_op jit(solution)/shard_map/ppermute | solution.py:12
  190.1 32.7 %collective-permute-start.12 = (f32[64,128]{1,0:T(8,128)S(1)}, f32[64,128]{1,0:T(8,128)S(1)}, u32[]{:S(2)}, u32[]{:S(2)}) collective-permute-start(f32[64,128]{1,0:T(8,128)S(1)} %get-tuple-element.55), channel_id=1, source_target_pairs={{252,0},{0,4},{4,8},{8,12},{12,16},{16,20},{20,24},{24,28},{28,32}... | collective-permute-start | bytes 98312 | tf_op jit(solution)/shard_map/ppermute | solution.py:12
  190.1 38.4 %collective-permute-start.13 = (f32[64,128]{1,0:T(8,128)}, f32[64,128]{1,0:T(8,128)S(1)}, u32[]{:S(2)}, u32[]{:S(2)}) collective-permute-start(f32[64,128]{1,0:T(8,128)} %get-tuple-element.54), channel_id=1, source_target_pairs={{4,0},{8,4},{12,8},{16,12},{20,16},{24,20},{28,24},{32,28},{36,32}... | collective-permute-start | bytes 98312 | tf_op jit(solution)/shard_map/ppermute | solution.py:12
  196.6 33.9 %collective-permute-start.14 = (f32[64,128]{1,0:T(8,128)}, f32[64,128]{1,0:T(8,128)}, u32[]{:S(2)}, u32[]{:S(2)}) collective-permute-start(f32[64,128]{1,0:T(8,128)} %get-tuple-element.53), channel_id=1, source_target_pairs={{248,0},{252,4},{0,8},{4,12},{8,16},{12,20},{16,24},{20,28},{24,32... | collective-permute-start | bytes 98312 | tf_op jit(solution)/shard_map/ppermute | solution.py:12
  198.1 39.6 %collective-permute-start.15 = (f32[64,128]{1,0:T(8,128)}, f32[64,128]{1,0:T(8,128)}, u32[]{:S(2)}, u32[]{:S(2)}) collective-permute-start(f32[64,128]{1,0:T(8,128)} %get-tuple-element.52), channel_id=1, source_target_pairs={{8,0},{12,4},{16,8},{20,12},{24,16},{28,20},{32,24},{36,28},{40,32... | collective-permute-start | bytes 98312 | tf_op jit(solution)/shard_map/ppermute | solution.py:12
  222.8 29.7 %collective-permute-start.44 = (f32[64,128]{0,1:T(8,128)}, f32[64,128]{0,1:T(8,128)}, u32[]{:S(2)}, u32[]{:S(2)}) collective-permute-start(f32[64,128]{0,1:T(8,128)} %get-tuple-element.23), channel_id=1, source_target_pairs={{252,0},{0,4},{4,8},{8,12},{12,16},{16,20},{20,24},{24,28},{28,32}... | collective-permute-start | bytes 98312 | tf_op jit(solution)/shard_map/ppermute | solution.py:12
  222.8 36.3 %collective-permute-start.45 = (f32[64,128]{0,1:T(8,128)}, f32[64,128]{0,1:T(8,128)S(1)}, u32[]{:S(2)}, u32[]{:S(2)}) collective-permute-start(f32[64,128]{0,1:T(8,128)} %get-tuple-element.22), channel_id=1, source_target_pairs={{4,0},{8,4},{12,8},{16,12},{20,16},{24,20},{28,24},{32,28},{36,32}... | collective-permute-start | bytes 98312 | tf_op jit(solution)/shard_map/ppermute | solution.py:12
  229.1 30.6 %collective-permute-start.46 = (f32[64,128]{0,1:T(8,128)}, f32[64,128]{0,1:T(8,128)S(1)}, u32[]{:S(2)}, u32[]{:S(2)}) collective-permute-start(f32[64,128]{0,1:T(8,128)} %get-tuple-element.21), channel_id=1, source_target_pairs={{248,0},{252,4},{0,8},{4,12},{8,16},{12,20},{16,24},{20,28},{24,32... | collective-permute-start | bytes 98312 | tf_op jit(solution)/shard_map/ppermute | solution.py:12
  230.5 35.3 %collective-permute-start.47 = (f32[64,128]{0,1:T(8,128)}, f32[64,128]{0,1:T(8,128)}, u32[]{:S(2)}, u32[]{:S(2)}) collective-permute-start(f32[64,128]{0,1:T(8,128)} %get-tuple-element.20), channel_id=1, source_target_pairs={{8,0},{12,4},{16,8},{20,12},{24,16},{28,20},{32,24},{36,28},{40,32... | collective-permute-start | bytes 98312 | tf_op jit(solution)/shard_map/ppermute | solution.py:12
  252.6 29.1 %collective-permute-start.16 = (f32[64,128]{1,0:T(8,128)}, f32[64,128]{1,0:T(8,128)}, u32[]{:S(2)}, u32[]{:S(2)}) collective-permute-start(f32[64,128]{1,0:T(8,128)} %get-tuple-element.51), channel_id=1, source_target_pairs={{252,0},{0,4},{4,8},{8,12},{12,16},{16,20},{20,24},{24,28},{28,32}... | collective-permute-start | bytes 98312 | tf_op jit(solution)/shard_map/ppermute | solution.py:12
  252.6 34.9 %collective-permute-start.17 = (f32[64,128]{1,0:T(8,128)}, f32[64,128]{1,0:T(8,128)}, u32[]{:S(2)}, u32[]{:S(2)}) collective-permute-start(f32[64,128]{1,0:T(8,128)} %get-tuple-element.50), channel_id=1, source_target_pairs={{4,0},{8,4},{12,8},{16,12},{20,16},{24,20},{28,24},{32,28},{36,32}... | collective-permute-start | bytes 98312 | tf_op jit(solution)/shard_map/ppermute | solution.py:12
  259.1 29.2 %collective-permute-start.18 = (f32[64,128]{1,0:T(8,128)}, f32[64,128]{1,0:T(8,128)}, u32[]{:S(2)}, u32[]{:S(2)}) collective-permute-start(f32[64,128]{1,0:T(8,128)} %get-tuple-element.49), channel_id=1, source_target_pairs={{248,0},{252,4},{0,8},{4,12},{8,16},{12,20},{16,24},{20,28},{24,32... | collective-permute-start | bytes 98312 | tf_op jit(solution)/shard_map/ppermute | solution.py:12
  259.7 34.8 %collective-permute-start.19 = (f32[64,128]{1,0:T(8,128)}, f32[64,128]{1,0:T(8,128)}, u32[]{:S(2)}, u32[]{:S(2)}) collective-permute-start(f32[64,128]{1,0:T(8,128)} %get-tuple-element.48), channel_id=1, source_target_pairs={{8,0},{12,4},{16,8},{20,12},{24,16},{28,20},{32,24},{36,28},{40,32... | collective-permute-start | bytes 98312 | tf_op jit(solution)/shard_map/ppermute | solution.py:12
  281.7 25.6 %collective-permute-start.48 = (f32[64,128]{0,1:T(8,128)}, f32[64,128]{0,1:T(8,128)}, u32[]{:S(2)}, u32[]{:S(2)}) collective-permute-start(f32[64,128]{0,1:T(8,128)} %get-tuple-element.19), channel_id=1, source_target_pairs={{252,0},{0,4},{4,8},{8,12},{12,16},{16,20},{20,24},{24,28},{28,32}... | collective-permute-start | bytes 98312 | tf_op jit(solution)/shard_map/ppermute | solution.py:12
  281.7 32.1 %collective-permute-start.49 = (f32[64,128]{0,1:T(8,128)}, f32[64,128]{0,1:T(8,128)S(1)}, u32[]{:S(2)}, u32[]{:S(2)}) collective-permute-start(f32[64,128]{0,1:T(8,128)} %get-tuple-element.18), channel_id=1, source_target_pairs={{4,0},{8,4},{12,8},{16,12},{20,16},{24,20},{28,24},{32,28},{36,32}... | collective-permute-start | bytes 98312 | tf_op jit(solution)/shard_map/ppermute | solution.py:12
  287.5 26.9 %collective-permute-start.50 = (f32[64,128]{0,1:T(8,128)}, f32[64,128]{0,1:T(8,128)S(1)}, u32[]{:S(2)}, u32[]{:S(2)}) collective-permute-start(f32[64,128]{0,1:T(8,128)} %get-tuple-element.17), channel_id=1, source_target_pairs={{248,0},{252,4},{0,8},{4,12},{8,16},{12,20},{16,24},{20,28},{24,32... | collective-permute-start | bytes 98312 | tf_op jit(solution)/shard_map/ppermute | solution.py:12
  288.3 32.4 %collective-permute-start.51 = (f32[64,128]{0,1:T(8,128)}, f32[64,128]{0,1:T(8,128)}, u32[]{:S(2)}, u32[]{:S(2)}) collective-permute-start(f32[64,128]{0,1:T(8,128)} %get-tuple-element.16), channel_id=1, source_target_pairs={{8,0},{12,4},{16,8},{20,12},{24,16},{28,20},{32,24},{36,28},{40,32... | collective-permute-start | bytes 98312 | tf_op jit(solution)/shard_map/ppermute | solution.py:12
  307.2 29.2 %collective-permute-start.20 = (f32[64,128]{1,0:T(8,128)S(1)}, f32[64,128]{1,0:T(8,128)S(1)}, u32[]{:S(2)}, u32[]{:S(2)}) collective-permute-start(f32[64,128]{1,0:T(8,128)S(1)} %get-tuple-element.47), channel_id=1, source_target_pairs={{252,0},{0,4},{4,8},{8,12},{12,16},{16,20},{20,24},{24,28},{28,32}... | collective-permute-start | bytes 98312 | tf_op jit(solution)/shard_map/ppermute | solution.py:12
  307.3 34.2 %collective-permute-start.21 = (f32[64,128]{1,0:T(8,128)S(1)}, f32[64,128]{1,0:T(8,128)S(1)}, u32[]{:S(2)}, u32[]{:S(2)}) collective-permute-start(f32[64,128]{1,0:T(8,128)S(1)} %get-tuple-element.46), channel_id=1, source_target_pairs={{4,0},{8,4},{12,8},{16,12},{20,16},{24,20},{28,24},{32,28},{36,32}... | collective-permute-start | bytes 98312 | tf_op jit(solution)/shard_map/ppermute | solution.py:12
  313.8 27.8 %collective-permute-start.22 = (f32[64,128]{1,0:T(8,128)S(1)}, f32[64,128]{1,0:T(8,128)S(1)}, u32[]{:S(2)}, u32[]{:S(2)}) collective-permute-start(f32[64,128]{1,0:T(8,128)S(1)} %get-tuple-element.45), channel_id=1, source_target_pairs={{248,0},{252,4},{0,8},{4,12},{8,16},{12,20},{16,24},{20,28},{24,32... | collective-permute-start | bytes 98312 | tf_op jit(solution)/shard_map/ppermute | solution.py:12
  314.4 33.0 %collective-permute-start.23 = (f32[64,128]{1,0:T(8,128)S(1)}, f32[64,128]{1,0:T(8,128)S(1)}, u32[]{:S(2)}, u32[]{:S(2)}) collective-permute-start(f32[64,128]{1,0:T(8,128)S(1)} %get-tuple-element.44), channel_id=1, source_target_pairs={{8,0},{12,4},{16,8},{20,12},{24,16},{28,20},{32,24},{36,28},{40,32... | collective-permute-start | bytes 98312 | tf_op jit(solution)/shard_map/ppermute | solution.py:12
  336.4 23.5 %collective-permute-start.52 = (f32[64,128]{0,1:T(8,128)}, f32[64,128]{0,1:T(8,128)}, u32[]{:S(2)}, u32[]{:S(2)}) collective-permute-start(f32[64,128]{0,1:T(8,128)} %get-tuple-element.15), channel_id=1, source_target_pairs={{252,0},{0,4},{4,8},{8,12},{12,16},{16,20},{20,24},{24,28},{28,32}... | collective-permute-start | bytes 98312 | tf_op jit(solution)/shard_map/ppermute | solution.py:12
  336.4 30.0 %collective-permute-start.53 = (f32[64,128]{0,1:T(8,128)}, f32[64,128]{0,1:T(8,128)S(1)}, u32[]{:S(2)}, u32[]{:S(2)}) collective-permute-start(f32[64,128]{0,1:T(8,128)} %get-tuple-element.14), channel_id=1, source_target_pairs={{4,0},{8,4},{12,8},{16,12},{20,16},{24,20},{28,24},{32,28},{36,32}... | collective-permute-start | bytes 98312 | tf_op jit(solution)/shard_map/ppermute | solution.py:12
  341.5 25.6 %collective-permute-start.54 = (f32[64,128]{0,1:T(8,128)}, f32[64,128]{0,1:T(8,128)S(1)}, u32[]{:S(2)}, u32[]{:S(2)}) collective-permute-start(f32[64,128]{0,1:T(8,128)} %get-tuple-element.13), channel_id=1, source_target_pairs={{248,0},{252,4},{0,8},{4,12},{8,16},{12,20},{16,24},{20,28},{24,32... | collective-permute-start | bytes 98312 | tf_op jit(solution)/shard_map/ppermute | solution.py:12
  341.6 31.6 %collective-permute-start.55 = (f32[64,128]{0,1:T(8,128)}, f32[64,128]{0,1:T(8,128)}, u32[]{:S(2)}, u32[]{:S(2)}) collective-permute-start(f32[64,128]{0,1:T(8,128)} %get-tuple-element.12), channel_id=1, source_target_pairs={{8,0},{12,4},{16,8},{20,12},{24,16},{28,20},{32,24},{36,28},{40,32... | collective-permute-start | bytes 98312 | tf_op jit(solution)/shard_map/ppermute | solution.py:12
  359.9 29.1 %collective-permute-start.24 = (f32[64,128]{1,0:T(8,128)}, f32[64,128]{1,0:T(8,128)}, u32[]{:S(2)}, u32[]{:S(2)}) collective-permute-start(f32[64,128]{1,0:T(8,128)} %get-tuple-element.43), channel_id=1, source_target_pairs={{252,0},{0,4},{4,8},{8,12},{12,16},{16,20},{20,24},{24,28},{28,32}... | collective-permute-start | bytes 98312 | tf_op jit(solution)/shard_map/ppermute | solution.py:12
  359.9 34.9 %collective-permute-start.25 = (f32[64,128]{1,0:T(8,128)}, f32[64,128]{1,0:T(8,128)}, u32[]{:S(2)}, u32[]{:S(2)}) collective-permute-start(f32[64,128]{1,0:T(8,128)} %get-tuple-element.42), channel_id=1, source_target_pairs={{4,0},{8,4},{12,8},{16,12},{20,16},{24,20},{28,24},{32,28},{36,32}... | collective-permute-start | bytes 98312 | tf_op jit(solution)/shard_map/ppermute | solution.py:12
  366.5 29.1 %collective-permute-start.26 = (f32[64,128]{1,0:T(8,128)}, f32[64,128]{1,0:T(8,128)}, u32[]{:S(2)}, u32[]{:S(2)}) collective-permute-start(f32[64,128]{1,0:T(8,128)} %get-tuple-element.41), channel_id=1, source_target_pairs={{248,0},{252,4},{0,8},{4,12},{8,16},{12,20},{16,24},{20,28},{24,32... | collective-permute-start | bytes 98312 | tf_op jit(solution)/shard_map/ppermute | solution.py:12
  367.1 34.8 %collective-permute-start.27 = (f32[64,128]{1,0:T(8,128)}, f32[64,128]{1,0:T(8,128)}, u32[]{:S(2)}, u32[]{:S(2)}) collective-permute-start(f32[64,128]{1,0:T(8,128)} %get-tuple-element.40), channel_id=1, source_target_pairs={{8,0},{12,4},{16,8},{20,12},{24,16},{28,20},{32,24},{36,28},{40,32... | collective-permute-start | bytes 98312 | tf_op jit(solution)/shard_map/ppermute | solution.py:12
  389.0 26.2 %collective-permute-start.56 = (f32[64,128]{0,1:T(8,128)}, f32[64,128]{0,1:T(8,128)}, u32[]{:S(2)}, u32[]{:S(2)}) collective-permute-start(f32[64,128]{0,1:T(8,128)} %get-tuple-element.11), channel_id=1, source_target_pairs={{252,0},{0,4},{4,8},{8,12},{12,16},{16,20},{20,24},{24,28},{28,32}... | collective-permute-start | bytes 98312 | tf_op jit(solution)/shard_map/ppermute | solution.py:12
  389.0 32.7 %collective-permute-start.57 = (f32[64,128]{0,1:T(8,128)}, f32[64,128]{0,1:T(8,128)S(1)}, u32[]{:S(2)}, u32[]{:S(2)}) collective-permute-start(f32[64,128]{0,1:T(8,128)} %get-tuple-element.10), channel_id=1, source_target_pairs={{4,0},{8,4},{12,8},{16,12},{20,16},{24,20},{28,24},{32,28},{36,32}... | collective-permute-start | bytes 98312 | tf_op jit(solution)/shard_map/ppermute | solution.py:12
  394.8 27.5 %collective-permute-start.58 = (f32[64,128]{0,1:T(8,128)}, f32[64,128]{0,1:T(8,128)S(1)}, u32[]{:S(2)}, u32[]{:S(2)}) collective-permute-start(f32[64,128]{0,1:T(8,128)} %get-tuple-element.9), channel_id=1, source_target_pairs={{248,0},{252,4},{0,8},{4,12},{8,16},{12,20},{16,24},{20,28},{24,32... | collective-permute-start | bytes 98312 | tf_op jit(solution)/shard_map/ppermute | solution.py:12
  395.6 33.0 %collective-permute-start.59 = (f32[64,128]{0,1:T(8,128)}, f32[64,128]{0,1:T(8,128)}, u32[]{:S(2)}, u32[]{:S(2)}) collective-permute-start(f32[64,128]{0,1:T(8,128)} %get-tuple-element.8), channel_id=1, source_target_pairs={{8,0},{12,4},{16,8},{20,12},{24,16},{28,20},{32,24},{36,28},{40,32... | collective-permute-start | bytes 98312 | tf_op jit(solution)/shard_map/ppermute | solution.py:12
  415.2 28.6 %collective-permute-start.28 = (f32[64,128]{1,0:T(8,128)}, f32[64,128]{1,0:T(8,128)}, u32[]{:S(2)}, u32[]{:S(2)}) collective-permute-start(f32[64,128]{1,0:T(8,128)} %get-tuple-element.39), channel_id=1, source_target_pairs={{252,0},{0,4},{4,8},{8,12},{12,16},{16,20},{20,24},{24,28},{28,32}... | collective-permute-start | bytes 98312 | tf_op jit(solution)/shard_map/ppermute | solution.py:12
  415.2 34.4 %collective-permute-start.29 = (f32[64,128]{1,0:T(8,128)}, f32[64,128]{1,0:T(8,128)}, u32[]{:S(2)}, u32[]{:S(2)}) collective-permute-start(f32[64,128]{1,0:T(8,128)} %get-tuple-element.38), channel_id=1, source_target_pairs={{4,0},{8,4},{12,8},{16,12},{20,16},{24,20},{28,24},{32,28},{36,32}... | collective-permute-start | bytes 98312 | tf_op jit(solution)/shard_map/ppermute | solution.py:12
  421.7 28.6 %collective-permute-start.30 = (f32[64,128]{1,0:T(8,128)}, f32[64,128]{1,0:T(8,128)}, u32[]{:S(2)}, u32[]{:S(2)}) collective-permute-start(f32[64,128]{1,0:T(8,128)} %get-tuple-element.37), channel_id=1, source_target_pairs={{248,0},{252,4},{0,8},{4,12},{8,16},{12,20},{16,24},{20,28},{24,32... | collective-permute-start | bytes 98312 | tf_op jit(solution)/shard_map/ppermute | solution.py:12
  422.4 34.4 %collective-permute-start.31 = (f32[64,128]{1,0:T(8,128)}, f32[64,128]{1,0:T(8,128)}, u32[]{:S(2)}, u32[]{:S(2)}) collective-permute-start(f32[64,128]{1,0:T(8,128)} %get-tuple-element.36), channel_id=1, source_target_pairs={{8,0},{12,4},{16,8},{20,12},{24,16},{28,20},{32,24},{36,28},{40,32... | collective-permute-start | bytes 98312 | tf_op jit(solution)/shard_map/ppermute | solution.py:12
  443.7 13.9 %collective-permute-start.60 = (f32[64,128]{0,1:T(8,128)S(1)}, f32[64,128]{0,1:T(8,128)S(1)}, u32[]{:S(2)}, u32[]{:S(2)}) collective-permute-start(f32[64,128]{0,1:T(8,128)S(1)} %get-tuple-element.7), channel_id=1, source_target_pairs={{252,0},{0,4},{4,8},{8,12},{12,16},{16,20},{20,24},{24,28},{28,32}... | collective-permute-start | bytes 98312 | tf_op jit(solution)/shard_map/ppermute | solution.py:12
  443.8 14.4 %collective-permute-start.61 = (f32[64,128]{0,1:T(8,128)S(1)}, f32[64,128]{0,1:T(8,128)S(1)}, u32[]{:S(2)}, u32[]{:S(2)}) collective-permute-start(f32[64,128]{0,1:T(8,128)S(1)} %get-tuple-element.6), channel_id=1, source_target_pairs={{4,0},{8,4},{12,8},{16,12},{20,16},{24,20},{28,24},{32,28},{36,32}... | collective-permute-start | bytes 98312 | tf_op jit(solution)/shard_map/ppermute | solution.py:12
  449.6 9.2 %collective-permute-start.62 = (f32[64,128]{0,1:T(8,128)S(1)}, f32[64,128]{0,1:T(8,128)S(1)}, u32[]{:S(2)}, u32[]{:S(2)}) collective-permute-start(f32[64,128]{0,1:T(8,128)S(1)} %get-tuple-element.5), channel_id=1, source_target_pairs={{248,0},{252,4},{0,8},{4,12},{8,16},{12,20},{16,24},{20,28},{24,32... | collective-permute-start | bytes 98312 | tf_op jit(solution)/shard_map/ppermute | solution.py:12
  450.4 11.1 %collective-permute-start.63 = (f32[64,128]{0,1:T(8,128)S(1)}, f32[64,128]{0,1:T(8,128)S(1)}, u32[]{:S(2)}, u32[]{:S(2)}) collective-permute-start(f32[64,128]{0,1:T(8,128)S(1)} %get-tuple-element.4), channel_id=1, source_target_pairs={{8,0},{12,4},{16,8},{20,12},{24,16},{28,20},{32,24},{36,28},{40,32... | collective-permute-start | bytes 98312 | tf_op jit(solution)/shard_map/ppermute | solution.py:12
  (17 other events, 160.7 us)
Sparse Core Ops, SparseCore 0:
  473.9 181.1 all-reduce.1
where the time goes:
time: 673 us; the launch traced here: 664 us
  waiting for transfers between devices  187 us (28%)
  starting transfers between devices  164 us (24%)
  matrix products  131 us (19%)
  local copies, waits for them, and re-layouts  127 us (19%)
  blocking collectives  26.5 us (4%)
  between operations  15.7 us (2%)
  other arithmetic  13 us (2%)
    psum x1, waiting for transfers between devices, local(): summed = lax.psum(local_grads, 'dom')  173 us
    ppermute x64, starting transfers between devices, from_behind(): return lax.ppermute(block, axis, route)  163 us
    dot_general x16, matrix products, apply_operator(): jnp.einsum('ctj,tjk->ctk', picked, tile_values, precision=lax.Precision.H...  107 us
    unnamed x82, local copies, waits for them, and re-layouts  37.6 us
    gather x16, local copies, waits for them, and re-layouts, apply_operator(): picked = jnp.take(blocks, tile_cols.reshape(-1), axis=1)  31.3 us
    gather x24, local copies, waits for them, and re-layouts, apply_operator(): outgoing = jnp.take(field_in, send_list[0], axis=1)  18 us
    concatenate x16, local copies, waits for them, and re-layouts, apply_operator(): extended = jnp.concatenate([field_in] + received, axis=1)  14.5 us
    ppermute x64, waiting for transfers between devices, from_behind(): return lax.ppermute(block, axis, route)  14 us
  transfers between devices with their start and end apart: 65, of which 4 were waited for; matrix products, arithmetic and copies ran while one was open for 36% of the time, Pallas kernels for 0%

commit v1 on v0

--- a/solution.py
+++ b/solution.py
@@ -4,6 +4,14 @@
 from jax.sharding import PartitionSpec as P
 
 NEIGHBOUR_SHIFTS = (1, -1, 2, -2)
+
+
+def gather_by_exchange(array, axis, dim):
+    size = lax.axis_size(axis)
+    repeats = [size if d == dim else 1 for d in range(array.ndim)]
+    return lax.all_to_all(
+        jnp.tile(array, repeats), axis, split_axis=dim, concat_axis=dim, tiled=True
+    )
 
 
 def from_behind(block, axis, distance):
@@ -44,7 +52,7 @@
 
     feat_all, cot_all = (
         lax.all_gather(features, "chan", axis=0, tiled=True),
-        lax.all_gather(cotangent, "chan", axis=0, tiled=True),
+        gather_by_exchange(cotangent, "chan", 0),
     )
     feat_wide = feat_all.astype(jnp.float32)
 

time: 673 us -> 611 us (0.908)
  local copies, waits for them, and re-layouts: 127 us -> 74.4 us
  blocking collectives: 26.5 us -> 13.4 us
  starting transfers between devices: 164 us -> 176 us
    unnamed x82 -> x80, local copies, waits for them, and re-layouts: 37.6 us -> 9.93 us
    all_gather x1 -> x0, blocking collectives: 13.7 us -> none  [local(): lax.all_gather(cotangent, 'chan', axis=0, tiled=True)]
    concatenate x16, local copies, waits for them, and re-layouts: 14.5 us -> 1.94 us  [apply_operator(): extended = jnp.concatenate([field_in] + received, axis=1)]
    psum x1, waiting for transfers between devices: 173 us -> 163 us  [local(): summed = lax.psum(local_grads, 'dom')]
    ppermute x64, waiting for transfers between devices: 14 us -> 22.3 us  [from_behind(): return lax.ppermute(block, axis, route)]
    squeeze x16, local copies, waits for them, and re-layouts: 8.17 us -> 0.91 us  [exchange_rows(): outgoing[:, slot_index]]
  transfers between devices with their start and end apart: 65 -> 66, of which waited for: 4 -> 18; matrix products, arithmetic and copies ran while one was open for 36% -> 26% of each run, Pallas kernels for 0% -> 0%
where the time goes in v1:
time: 611 us; the launch traced here: 602 us
  waiting for transfers between devices  185 us (30%)
  starting transfers between devices  176 us (29%)
  matrix products  126 us (21%)
  local copies, waits for them, and re-layouts  74.4 us (12%)
  between operations  15.8 us (3%)
  blocking collectives  13.4 us (2%)
  other arithmetic  11.6 us (2%)
    ppermute x64, starting transfers between devices, from_behind(): return lax.ppermute(block, axis, route)  170 us
    psum x1, waiting for transfers between devices, local(): summed = lax.psum(local_grads, 'dom')  163 us
    dot_general x16, matrix products, apply_operator(): jnp.einsum('ctj,tjk->ctk', picked, tile_values, precision=lax.Precision.H...  104 us
    gather x16, local copies, waits for them, and re-layouts, apply_operator(): picked = jnp.take(blocks, tile_cols.reshape(-1), axis=1)  27.1 us
    ppermute x64, waiting for transfers between devices, from_behind(): return lax.ppermute(block, axis, route)  22.3 us
    gather x24, local copies, waits for them, and re-layouts, apply_operator(): outgoing = jnp.take(field_in, send_list[0], axis=1)  20.6 us
    all_gather x1, blocking collectives, local(): lax.all_gather(features, 'chan', axis=0, tiled=True)  13.4 us
  transfers between devices with their start and end apart: 66, of which 18 were waited for; matrix products, arithmetic and copies ran while one was open for 26% of the time, Pallas kernels for 0%

profile of v1, /device:TPU:2, one launch (start us, length us, event | category | flops | bytes accessed | tf_op | source)
XLA Modules:
  0.0 602.3 jit_solution(6355846648055474403)
XLA Ops:
  9.0 5.7 all-to-all-start
  18.6 6.4 %collective-permute-start.33 = (f32[64,128]{0,1:T(8,128)S(1)}, f32[64,128]{0,1:T(8,128)S(1)}, u32[]{:S(2)}, u32[]{:S(2)}) collective-permute-start(f32[64,128]{0,1:T(8,128)S(1)} %get-tuple-element.34), channel_id=1, source_target_pairs={{4,0},{8,4},{12,8},{16,12},{20,16},{24,20},{28,24},{32,28},{36,32}... | collective-permute-start | bytes 98312 | tf_op jit(solution)/shard_map/ppermute | solution.py:20
  25.0 5.3 collective-permute-start.35
  30.4 13.4 %all_gather.3 = bf16[256,1024]{1,0:T(8,128)(2,1)S(1)} all-gather(bf16[64,1024]{1,0:T(8,128)(2,1)S(1)} %copy-done.13), channel_id=1, replica_groups=mesh['dom'=64,'chan'=4] {'chan'}, dimensions={0}, use_global_device_ids=true | all-gather | bytes 655360 | tf_op jit(solution)/shard_map/all_gather | solution.py:54
  45.8 6.4 %bitcast_reduce_fusion.7 = f32[64,8,128]{2,0,1:T(8,128)} fusion(f32[64,128,128]{2,1,0:T(8,128)} %param.13, f32[64,64,128]{2,1,0:T(8,128)S(1)} %gather_fusion.17, pred[64]{0:T(512)(128)(4,1)S(1)} %compare_and_fusion), kind=kOutput, calls=%fused_computation.39 | convolution fusion | flops 806289408 | bytes 6553664 | tf_op jit(solution)/shard_map/ctj,tjk->ctk/dot_general | solution.py:40
  55.9 5.1 collective-permute-start.37
  61.1 5.5 collective-permute-start.39
  66.6 2.1 collective-permute-done.38
  68.9 2.0 gather_fusion.19
  71.0 6.7 %bitcast_reduce_fusion.6 = f32[64,8,128]{2,0,1:T(8,128)S(1)} fusion(f32[64,128,128]{2,1,0:T(8,128)} %param.13, f32[64,64,128]{2,1,0:T(8,128)} %gather_fusion.19, pred[64]{0:T(512)(128)(4,1)S(1)} %compare_and_fusion), kind=kOutput, calls=%fused_computation.38 | convolution fusion | flops 806289408 | bytes 6553664 | tf_op jit(solution)/shard_map/ctj,tjk->ctk/dot_general | solution.py:40
  82.4 5.0 collective-permute-start.41
  87.5 5.5 collective-permute-start.43
  95.3 2.0 gather_fusion.21
  97.3 6.7 %bitcast_reduce_fusion.5 = f32[64,8,128]{2,0,1:T(8,128)S(1)} fusion(f32[64,128,128]{2,1,0:T(8,128)} %param.13, f32[64,64,128]{2,1,0:T(8,128)} %gather_fusion.21, pred[64]{0:T(512)(128)(4,1)S(1)} %compare_and_fusion), kind=kOutput, calls=%fused_computation.37 | convolution fusion | flops 806289408 | bytes 6553664 | tf_op jit(solution)/shard_map/ctj,tjk->ctk/dot_general | solution.py:40
  108.8 5.0 collective-permute-start.45
  113.8 5.6 collective-permute-start.47
  121.7 2.0 gather_fusion.23
  123.7 6.7 %bitcast_reduce_fusion.4 = f32[64,8,128]{2,0,1:T(8,128)S(1)} fusion(f32[64,128,128]{2,1,0:T(8,128)} %param.13, f32[64,64,128]{2,1,0:T(8,128)} %gather_fusion.23, pred[64]{0:T(512)(128)(4,1)S(1)} %compare_and_fusion), kind=kOutput, calls=%fused_computation.36 | convolution fusion | flops 806289408 | bytes 6553664 | tf_op jit(solution)/shard_map/ctj,tjk->ctk/dot_general | solution.py:40
  134.1 5.0 collective-permute-start.49
  139.1 5.8 collective-permute-start.51
  149.3 2.0 gather_fusion.25
  151.4 6.7 %bitcast_reduce_fusion.3 = f32[64,8,128]{2,0,1:T(8,128)S(1)} fusion(f32[64,128,128]{2,1,0:T(8,128)} %param.13, f32[64,64,128]{2,1,0:T(8,128)} %gather_fusion.25, pred[64]{0:T(512)(128)(4,1)S(1)} %compare_and_fusion), kind=kOutput, calls=%fused_computation.35 | convolution fusion | flops 806289408 | bytes 6553664 | tf_op jit(solution)/shard_map/ctj,tjk->ctk/dot_general | solution.py:40
  161.7 5.0 collective-permute-start.53
  166.8 5.5 collective-permute-start.55
  177.0 2.0 gather_fusion.27
  179.0 6.7 %bitcast_reduce_fusion.2 = f32[64,8,128]{2,0,1:T(8,128)S(1)} fusion(f32[64,128,128]{2,1,0:T(8,128)} %param.13, f32[64,64,128]{2,1,0:T(8,128)} %gather_fusion.27, pred[64]{0:T(512)(128)(4,1)S(1)} %compare_and_fusion), kind=kOutput, calls=%fused_computation.34 | convolution fusion | flops 806289408 | bytes 6553664 | tf_op jit(solution)/shard_map/ctj,tjk->ctk/dot_general | solution.py:40
  189.4 5.0 collective-permute-start.57
  194.4 5.5 collective-permute-start.59
  202.3 2.0 gather_fusion.29
  204.3 6.7 %bitcast_reduce_fusion.1 = f32[64,8,128]{2,0,1:T(8,128)S(1)} fusion(f32[64,128,128]{2,1,0:T(8,128)} %param.13, f32[64,64,128]{2,1,0:T(8,128)} %gather_fusion.29, pred[64]{0:T(512)(128)(4,1)S(1)} %compare_and_fusion), kind=kOutput, calls=%fused_computation.33 | convolution fusion | flops 806289408 | bytes 6553664 | tf_op jit(solution)/shard_map/ctj,tjk->ctk/dot_general | solution.py:40
  216.3 5.1 collective-permute-start.61
  221.3 5.3 collective-permute-start.63
  231.5 5.0 collective-permute-start.1
  236.7 5.6 collective-permute-start.3
  243.9 2.0 gather_fusion.1
  246.0 6.7 %bitcast_reduce_fusion.15 = f32[64,8,128]{2,0,1:T(8,128)S(1)} fusion(f32[64,128,128]{2,1,0:T(8,128)} %param.13, f32[64,64,128]{2,1,0:T(8,128)} %gather_fusion.1, pred[64]{0:T(512)(128)(4,1)S(1)} %compare_and_fusion), kind=kOutput, calls=%fused_computation.47 | convolution fusion | flops 806289408 | bytes 6553664 | tf_op jit(solution)/shard_map/ctj,tjk->ctk/dot_general | solution.py:40
  255.8 5.0 collective-permute-start.5
  260.8 5.5 collective-permute-start.7
  268.1 2.0 gather_fusion.3
  270.1 6.7 %bitcast_reduce_fusion.14 = f32[64,8,128]{2,0,1:T(8,128)S(1)} fusion(f32[64,128,128]{2,1,0:T(8,128)} %param.13, f32[64,64,128]{2,1,0:T(8,128)} %gather_fusion.3, pred[64]{0:T(512)(128)(4,1)S(1)} %compare_and_fusion), kind=kOutput, calls=%fused_computation.46 | convolution fusion | flops 806289408 | bytes 6553664 | tf_op jit(solution)/shard_map/ctj,tjk->ctk/dot_general | solution.py:40
  281.9 2.0 gather_fusion.31
  283.9 5.0 collective-permute-start.9
  289.0 5.5 collective-permute-start.11
  296.2 2.0 gather_fusion.5
  298.3 6.7 %bitcast_reduce_fusion.13 = f32[64,8,128]{2,0,1:T(8,128)S(1)} fusion(f32[64,128,128]{2,1,0:T(8,128)} %param.13, f32[64,64,128]{2,1,0:T(8,128)} %gather_fusion.5, pred[64]{0:T(512)(128)(4,1)S(1)} %compare_and_fusion), kind=kOutput, calls=%fused_computation.45 | convolution fusion | flops 806289408 | bytes 6553664 | tf_op jit(solution)/shard_map/ctj,tjk->ctk/dot_general | solution.py:40
  307.5 6.7 %bitcast_reduce_fusion = f32[64,8,128]{2,0,1:T(8,128)S(1)} fusion(f32[64,128,128]{2,1,0:T(8,128)} %param.13, f32[64,64,128]{2,1,0:T(8,128)} %gather_fusion.31, pred[64]{0:T(512)(128)(4,1)S(1)} %compare_and_fusion), kind=kOutput, calls=%fused_computation.32 | convolution fusion | flops 806289408 | bytes 6553664 | tf_op jit(solution)/shard_map/ctj,tjk->ctk/dot_general | solution.py:40
  314.2 5.1 collective-permute-start.13
  319.3 5.7 collective-permute-start.15
  326.7 2.0 gather_fusion.7
  328.7 6.7 %bitcast_reduce_fusion.12 = f32[64,8,128]{2,0,1:T(8,128)S(1)} fusion(f32[64,128,128]{2,1,0:T(8,128)} %param.13, f32[64,64,128]{2,1,0:T(8,128)} %gather_fusion.7, pred[64]{0:T(512)(128)(4,1)S(1)} %compare_and_fusion), kind=kOutput, calls=%fused_computation.44 | convolution fusion | flops 806289408 | bytes 6553664 | tf_op jit(solution)/shard_map/ctj,tjk->ctk/dot_general | solution.py:40
  338.8 5.1 collective-permute-start.17
  344.0 5.5 collective-permute-start.19
  353.5 2.0 gather_fusion.9
  355.5 6.7 %bitcast_reduce_fusion.11 = f32[64,8,128]{2,0,1:T(8,128)S(1)} fusion(f32[64,128,128]{2,1,0:T(8,128)} %param.13, f32[64,64,128]{2,1,0:T(8,128)} %gather_fusion.9, pred[64]{0:T(512)(128)(4,1)S(1)} %compare_and_fusion), kind=kOutput, calls=%fused_computation.43 | convolution fusion | flops 806289408 | bytes 6553664 | tf_op jit(solution)/shard_map/ctj,tjk->ctk/dot_general | solution.py:40
  367.8 5.1 collective-permute-start.21
  372.9 5.3 collective-permute-start.23
  380.9 5.7 bitcast_reduce_fusion.10
  390.4 5.3 collective-permute-start.25
  395.7 5.3 collective-permute-start.27
  403.7 5.7 bitcast_reduce_fusion.9
  411.9 162.8 %all-reduce.2.cloned.1.call-done = f32[9,256,64]{1,2,0:T(8,128)} async-done(((f32[9,256,64]{1,2,0:T(8,128)}), f32[9,256,64]{1,2,0:T(8,128)}) %all-reduce.2.cloned.1.call-update) | async-done | bytes 589840 | tf_op jit(solution)/shard_map/psum | solution.py:83
  576.6 3.3 collective-permute-start.29
  579.9 5.3 collective-permute-start.31
  587.9 5.7 bitcast_reduce_fusion.8
  (328 shorter events, 105.5 us)
Async XLA Ops:
  9.0 217.8 %all-to-all-start = ((bf16[4,64,1024]{2,1,0:T(8,128)(2,1)}), bf16[4,64,1024]{2,1,0:T(8,128)(2,1)S(1)}, u32[]{:S(2)}, u32[]{:S(2)}) async-start(bf16[4,64,1024]{2,1,0:T(8,128)(2,1)} %tile.2), calls=%async_computation | async-start | bytes 1048576 | tf_op jit(solution)/shard_map/all_to_all | solution.py:12
  14.7 560.0 %all-reduce.2.cloned.1.call-start = ((), (), s32[]{:S(2)}) async-start(), calls=%async_computation.1 | async-start | bytes 1179648 | tf_op jit(solution)/shard_map/psum | solution.py:83
  18.5 26.3 %collective-permute-start.32 = (f32[64,128]{0,1:T(8,128)S(1)}, f32[64,128]{0,1:T(8,128)S(1)}, u32[]{:S(2)}, u32[]{:S(2)}) collective-permute-start(f32[64,128]{0,1:T(8,128)S(1)} %get-tuple-element.35), channel_id=1, source_target_pairs={{252,0},{0,4},{4,8},{8,12},{12,16},{16,20},{20,24},{24,28},{28,32}... | collective-permute-start | bytes 98312 | tf_op jit(solution)/shard_map/ppermute | solution.py:20
  18.6 26.2 %collective-permute-start.33 = (f32[64,128]{0,1:T(8,128)S(1)}, f32[64,128]{0,1:T(8,128)S(1)}, u32[]{:S(2)}, u32[]{:S(2)}) collective-permute-start(f32[64,128]{0,1:T(8,128)S(1)} %get-tuple-element.34), channel_id=1, source_target_pairs={{4,0},{8,4},{12,8},{16,12},{20,16},{24,20},{28,24},{32,28},{36,32}... | collective-permute-start | bytes 98312 | tf_op jit(solution)/shard_map/ppermute | solution.py:20
  25.0 19.8 %collective-permute-start.34 = (f32[64,128]{0,1:T(8,128)S(1)}, f32[64,128]{0,1:T(8,128)S(1)}, u32[]{:S(2)}, u32[]{:S(2)}) collective-permute-start(f32[64,128]{0,1:T(8,128)S(1)} %get-tuple-element.33), channel_id=1, source_target_pairs={{248,0},{252,4},{0,8},{4,12},{8,16},{12,20},{16,24},{20,28},{24,32... | collective-permute-start | bytes 98312 | tf_op jit(solution)/shard_map/ppermute | solution.py:20
  25.0 19.8 %collective-permute-start.35 = (f32[64,128]{0,1:T(8,128)S(1)}, f32[64,128]{0,1:T(8,128)S(1)}, u32[]{:S(2)}, u32[]{:S(2)}) collective-permute-start(f32[64,128]{0,1:T(8,128)S(1)} %get-tuple-element.32), channel_id=1, source_target_pairs={{8,0},{12,4},{16,8},{20,12},{24,16},{28,20},{32,24},{36,28},{40,32... | collective-permute-start | bytes 98312 | tf_op jit(solution)/shard_map/ppermute | solution.py:20
  55.8 10.8 %collective-permute-start.36 = (f32[64,128]{0,1:T(8,128)S(1)}, f32[64,128]{0,1:T(8,128)S(1)}, u32[]{:S(2)}, u32[]{:S(2)}) collective-permute-start(f32[64,128]{0,1:T(8,128)S(1)} %get-tuple-element.31), channel_id=1, source_target_pairs={{252,0},{0,4},{4,8},{8,12},{12,16},{16,20},{20,24},{24,28},{28,32}... | collective-permute-start | bytes 98312 | tf_op jit(solution)/shard_map/ppermute | solution.py:20
  55.9 10.6 %collective-permute-start.37 = (f32[64,128]{0,1:T(8,128)S(1)}, f32[64,128]{0,1:T(8,128)S(1)}, u32[]{:S(2)}, u32[]{:S(2)}) collective-permute-start(f32[64,128]{0,1:T(8,128)S(1)} %get-tuple-element.30), channel_id=1, source_target_pairs={{4,0},{8,4},{12,8},{16,12},{20,16},{24,20},{28,24},{32,28},{36,32}... | collective-permute-start | bytes 98312 | tf_op jit(solution)/shard_map/ppermute | solution.py:20
  61.1 7.6 %collective-permute-start.38 = (f32[64,128]{0,1:T(8,128)S(1)}, f32[64,128]{0,1:T(8,128)S(1)}, u32[]{:S(2)}, u32[]{:S(2)}) collective-permute-start(f32[64,128]{0,1:T(8,128)S(1)} %get-tuple-element.29), channel_id=1, source_target_pairs={{248,0},{252,4},{0,8},{4,12},{8,16},{12,20},{16,24},{20,28},{24,32... | collective-permute-start | bytes 98312 | tf_op jit(solution)/shard_map/ppermute | solution.py:20
  61.1 7.6 %collective-permute-start.39 = (f32[64,128]{0,1:T(8,128)S(1)}, f32[64,128]{0,1:T(8,128)S(1)}, u32[]{:S(2)}, u32[]{:S(2)}) collective-permute-start(f32[64,128]{0,1:T(8,128)S(1)} %get-tuple-element.28), channel_id=1, source_target_pairs={{8,0},{12,4},{16,8},{20,12},{24,16},{28,20},{32,24},{36,28},{40,32... | collective-permute-start | bytes 98312 | tf_op jit(solution)/shard_map/ppermute | solution.py:20
  81.1 11.9 %collective-permute-start.40 = (f32[64,128]{0,1:T(8,128)S(1)}, f32[64,128]{0,1:T(8,128)S(1)}, u32[]{:S(2)}, u32[]{:S(2)}) collective-permute-start(f32[64,128]{0,1:T(8,128)S(1)} %get-tuple-element.27), channel_id=1, source_target_pairs={{252,0},{0,4},{4,8},{8,12},{12,16},{16,20},{20,24},{24,28},{28,32}... | collective-permute-start | bytes 98312 | tf_op jit(solution)/shard_map/ppermute | solution.py:20
  82.4 10.6 %collective-permute-start.41 = (f32[64,128]{0,1:T(8,128)S(1)}, f32[64,128]{0,1:T(8,128)S(1)}, u32[]{:S(2)}, u32[]{:S(2)}) collective-permute-start(f32[64,128]{0,1:T(8,128)S(1)} %get-tuple-element.26), channel_id=1, source_target_pairs={{4,0},{8,4},{12,8},{16,12},{20,16},{24,20},{28,24},{32,28},{36,32}... | collective-permute-start | bytes 98312 | tf_op jit(solution)/shard_map/ppermute | solution.py:20
  87.4 7.6 %collective-permute-start.42 = (f32[64,128]{0,1:T(8,128)S(1)}, f32[64,128]{0,1:T(8,128)S(1)}, u32[]{:S(2)}, u32[]{:S(2)}) collective-permute-start(f32[64,128]{0,1:T(8,128)S(1)} %get-tuple-element.25), channel_id=1, source_target_pairs={{248,0},{252,4},{0,8},{4,12},{8,16},{12,20},{16,24},{20,28},{24,32... | collective-permute-start | bytes 98312 | tf_op jit(solution)/shard_map/ppermute | solution.py:20
  87.5 7.6 %collective-permute-start.43 = (f32[64,128]{0,1:T(8,128)S(1)}, f32[64,128]{0,1:T(8,128)S(1)}, u32[]{:S(2)}, u32[]{:S(2)}) collective-permute-start(f32[64,128]{0,1:T(8,128)S(1)} %get-tuple-element.24), channel_id=1, source_target_pairs={{8,0},{12,4},{16,8},{20,12},{24,16},{28,20},{32,24},{36,28},{40,32... | collective-permute-start | bytes 98312 | tf_op jit(solution)/shard_map/ppermute | solution.py:20
  107.5 11.9 %collective-permute-start.44 = (f32[64,128]{0,1:T(8,128)S(1)}, f32[64,128]{0,1:T(8,128)S(1)}, u32[]{:S(2)}, u32[]{:S(2)}) collective-permute-start(f32[64,128]{0,1:T(8,128)S(1)} %get-tuple-element.23), channel_id=1, source_target_pairs={{252,0},{0,4},{4,8},{8,12},{12,16},{16,20},{20,24},{24,28},{28,32}... | collective-permute-start | bytes 98312 | tf_op jit(solution)/shard_map/ppermute | solution.py:20
  108.8 10.6 %collective-permute-start.45 = (f32[64,128]{0,1:T(8,128)S(1)}, f32[64,128]{0,1:T(8,128)S(1)}, u32[]{:S(2)}, u32[]{:S(2)}) collective-permute-start(f32[64,128]{0,1:T(8,128)S(1)} %get-tuple-element.22), channel_id=1, source_target_pairs={{4,0},{8,4},{12,8},{16,12},{20,16},{24,20},{28,24},{32,28},{36,32}... | collective-permute-start | bytes 98312 | tf_op jit(solution)/shard_map/ppermute | solution.py:20
  113.8 7.6 %collective-permute-start.46 = (f32[64,128]{0,1:T(8,128)S(1)}, f32[64,128]{0,1:T(8,128)S(1)}, u32[]{:S(2)}, u32[]{:S(2)}) collective-permute-start(f32[64,128]{0,1:T(8,128)S(1)} %get-tuple-element.21), channel_id=1, source_target_pairs={{248,0},{252,4},{0,8},{4,12},{8,16},{12,20},{16,24},{20,28},{24,32... | collective-permute-start | bytes 98312 | tf_op jit(solution)/shard_map/ppermute | solution.py:20
  113.8 7.6 %collective-permute-start.47 = (f32[64,128]{0,1:T(8,128)S(1)}, f32[64,128]{0,1:T(8,128)S(1)}, u32[]{:S(2)}, u32[]{:S(2)}) collective-permute-start(f32[64,128]{0,1:T(8,128)S(1)} %get-tuple-element.20), channel_id=1, source_target_pairs={{8,0},{12,4},{16,8},{20,12},{24,16},{28,20},{32,24},{36,28},{40,32... | collective-permute-start | bytes 98312 | tf_op jit(solution)/shard_map/ppermute | solution.py:20
  132.7 12.2 %collective-permute-start.48 = (f32[64,128]{0,1:T(8,128)S(1)}, f32[64,128]{0,1:T(8,128)S(1)}, u32[]{:S(2)}, u32[]{:S(2)}) collective-permute-start(f32[64,128]{0,1:T(8,128)S(1)} %get-tuple-element.19), channel_id=1, source_target_pairs={{252,0},{0,4},{4,8},{8,12},{12,16},{16,20},{20,24},{24,28},{28,32}... | collective-permute-start | bytes 98312 | tf_op jit(solution)/shard_map/ppermute | solution.py:20
  134.1 11.5 %collective-permute-start.49 = (f32[64,128]{0,1:T(8,128)S(1)}, f32[64,128]{0,1:T(8,128)S(1)}, u32[]{:S(2)}, u32[]{:S(2)}) collective-permute-start(f32[64,128]{0,1:T(8,128)S(1)} %get-tuple-element.18), channel_id=1, source_target_pairs={{4,0},{8,4},{12,8},{16,12},{20,16},{24,20},{28,24},{32,28},{36,32}... | collective-permute-start | bytes 98312 | tf_op jit(solution)/shard_map/ppermute | solution.py:20
  139.1 7.6 %collective-permute-start.50 = (f32[64,128]{0,1:T(8,128)S(1)}, f32[64,128]{0,1:T(8,128)S(1)}, u32[]{:S(2)}, u32[]{:S(2)}) collective-permute-start(f32[64,128]{0,1:T(8,128)S(1)} %get-tuple-element.17), channel_id=1, source_target_pairs={{248,0},{252,4},{0,8},{4,12},{8,16},{12,20},{16,24},{20,28},{24,32... | collective-permute-start | bytes 98312 | tf_op jit(solution)/shard_map/ppermute | solution.py:20
  139.1 8.2 %collective-permute-start.51 = (f32[64,128]{0,1:T(8,128)S(1)}, f32[64,128]{0,1:T(8,128)S(1)}, u32[]{:S(2)}, u32[]{:S(2)}) collective-permute-start(f32[64,128]{0,1:T(8,128)S(1)} %get-tuple-element.16), channel_id=1, source_target_pairs={{8,0},{12,4},{16,8},{20,12},{24,16},{28,20},{32,24},{36,28},{40,32... | collective-permute-start | bytes 98312 | tf_op jit(solution)/shard_map/ppermute | solution.py:20
  160.4 11.9 %collective-permute-start.52 = (f32[64,128]{0,1:T(8,128)S(1)}, f32[64,128]{0,1:T(8,128)S(1)}, u32[]{:S(2)}, u32[]{:S(2)}) collective-permute-start(f32[64,128]{0,1:T(8,128)S(1)} %get-tuple-element.15), channel_id=1, source_target_pairs={{252,0},{0,4},{4,8},{8,12},{12,16},{16,20},{20,24},{24,28},{28,32}... | collective-permute-start | bytes 98312 | tf_op jit(solution)/shard_map/ppermute | solution.py:20
  161.7 11.2 %collective-permute-start.53 = (f32[64,128]{0,1:T(8,128)S(1)}, f32[64,128]{0,1:T(8,128)S(1)}, u32[]{:S(2)}, u32[]{:S(2)}) collective-permute-start(f32[64,128]{0,1:T(8,128)S(1)} %get-tuple-element.14), channel_id=1, source_target_pairs={{4,0},{8,4},{12,8},{16,12},{20,16},{24,20},{28,24},{32,28},{36,32}... | collective-permute-start | bytes 98312 | tf_op jit(solution)/shard_map/ppermute | solution.py:20
  166.8 7.6 %collective-permute-start.54 = (f32[64,128]{0,1:T(8,128)S(1)}, f32[64,128]{0,1:T(8,128)S(1)}, u32[]{:S(2)}, u32[]{:S(2)}) collective-permute-start(f32[64,128]{0,1:T(8,128)S(1)} %get-tuple-element.13), channel_id=1, source_target_pairs={{248,0},{252,4},{0,8},{4,12},{8,16},{12,20},{16,24},{20,28},{24,32... | collective-permute-start | bytes 98312 | tf_op jit(solution)/shard_map/ppermute | solution.py:20
  166.8 8.2 %collective-permute-start.55 = (f32[64,128]{0,1:T(8,128)S(1)}, f32[64,128]{0,1:T(8,128)S(1)}, u32[]{:S(2)}, u32[]{:S(2)}) collective-permute-start(f32[64,128]{0,1:T(8,128)S(1)} %get-tuple-element.12), channel_id=1, source_target_pairs={{8,0},{12,4},{16,8},{20,12},{24,16},{28,20},{32,24},{36,28},{40,32... | collective-permute-start | bytes 98312 | tf_op jit(solution)/shard_map/ppermute | solution.py:20
  188.1 11.9 %collective-permute-start.56 = (f32[64,128]{0,1:T(8,128)S(1)}, f32[64,128]{0,1:T(8,128)S(1)}, u32[]{:S(2)}, u32[]{:S(2)}) collective-permute-start(f32[64,128]{0,1:T(8,128)S(1)} %get-tuple-element.11), channel_id=1, source_target_pairs={{252,0},{0,4},{4,8},{8,12},{12,16},{16,20},{20,24},{24,28},{28,32}... | collective-permute-start | bytes 98312 | tf_op jit(solution)/shard_map/ppermute | solution.py:20
  189.4 10.6 %collective-permute-start.57 = (f32[64,128]{0,1:T(8,128)S(1)}, f32[64,128]{0,1:T(8,128)S(1)}, u32[]{:S(2)}, u32[]{:S(2)}) collective-permute-start(f32[64,128]{0,1:T(8,128)S(1)} %get-tuple-element.10), channel_id=1, source_target_pairs={{4,0},{8,4},{12,8},{16,12},{20,16},{24,20},{28,24},{32,28},{36,32}... | collective-permute-start | bytes 98312 | tf_op jit(solution)/shard_map/ppermute | solution.py:20
  194.4 7.6 %collective-permute-start.58 = (f32[64,128]{0,1:T(8,128)S(1)}, f32[64,128]{0,1:T(8,128)S(1)}, u32[]{:S(2)}, u32[]{:S(2)}) collective-permute-start(f32[64,128]{0,1:T(8,128)S(1)} %get-tuple-element.9), channel_id=1, source_target_pairs={{248,0},{252,4},{0,8},{4,12},{8,16},{12,20},{16,24},{20,28},{24,32... | collective-permute-start | bytes 98312 | tf_op jit(solution)/shard_map/ppermute | solution.py:20
  194.4 7.6 %collective-permute-start.59 = (f32[64,128]{0,1:T(8,128)S(1)}, f32[64,128]{0,1:T(8,128)S(1)}, u32[]{:S(2)}, u32[]{:S(2)}) collective-permute-start(f32[64,128]{0,1:T(8,128)S(1)} %get-tuple-element.8), channel_id=1, source_target_pairs={{8,0},{12,4},{16,8},{20,12},{24,16},{28,20},{32,24},{36,28},{40,32... | collective-permute-start | bytes 98312 | tf_op jit(solution)/shard_map/ppermute | solution.py:20
  215.1 11.6 %collective-permute-start.60 = (f32[64,128]{0,1:T(8,128)S(1)}, f32[64,128]{0,1:T(8,128)S(1)}, u32[]{:S(2)}, u32[]{:S(2)}) collective-permute-start(f32[64,128]{0,1:T(8,128)S(1)} %get-tuple-element.7), channel_id=1, source_target_pairs={{252,0},{0,4},{4,8},{8,12},{12,16},{16,20},{20,24},{24,28},{28,32}... | collective-permute-start | bytes 98312 | tf_op jit(solution)/shard_map/ppermute | solution.py:20
  216.3 13.8 %collective-permute-start.61 = (f32[64,128]{0,1:T(8,128)}, f32[64,128]{0,1:T(8,128)}, u32[]{:S(2)}, u32[]{:S(2)}) collective-permute-start(f32[64,128]{0,1:T(8,128)} %get-tuple-element.6), channel_id=1, source_target_pairs={{4,0},{8,4},{12,8},{16,12},{20,16},{24,20},{28,24},{32,28},{36,32}... | collective-permute-start | bytes 98312 | tf_op jit(solution)/shard_map/ppermute | solution.py:20
  221.3 33.8 %collective-permute-start.62 = (f32[64,128]{0,1:T(8,128)}, f32[64,128]{0,1:T(8,128)S(1)}, u32[]{:S(2)}, u32[]{:S(2)}) collective-permute-start(f32[64,128]{0,1:T(8,128)} %get-tuple-element.5), channel_id=1, source_target_pairs={{248,0},{252,4},{0,8},{4,12},{8,16},{12,20},{16,24},{20,28},{24,32... | collective-permute-start | bytes 98312 | tf_op jit(solution)/shard_map/ppermute | solution.py:20
  221.3 60.2 %collective-permute-start.63 = (f32[64,128]{0,1:T(8,128)}, f32[64,128]{0,1:T(8,128)S(1)}, u32[]{:S(2)}, u32[]{:S(2)}) collective-permute-start(f32[64,128]{0,1:T(8,128)} %get-tuple-element.4), channel_id=1, source_target_pairs={{8,0},{12,4},{16,8},{20,12},{24,16},{28,20},{32,24},{36,28},{40,32... | collective-permute-start | bytes 98312 | tf_op jit(solution)/shard_map/ppermute | solution.py:20
  231.5 10.8 %collective-permute-start.1 = (f32[64,128]{1,0:T(8,128)S(1)}, f32[64,128]{1,0:T(8,128)S(1)}, u32[]{:S(2)}, u32[]{:S(2)}) collective-permute-start(f32[64,128]{1,0:T(8,128)S(1)} %get-tuple-element.66), channel_id=1, source_target_pairs={{4,0},{8,4},{12,8},{16,12},{20,16},{24,20},{28,24},{32,28},{36,32}... | collective-permute-start | bytes 98312 | tf_op jit(solution)/shard_map/ppermute | solution.py:20
  236.6 7.2 %collective-permute-start.2 = (f32[64,128]{1,0:T(8,128)S(1)}, f32[64,128]{1,0:T(8,128)S(1)}, u32[]{:S(2)}, u32[]{:S(2)}) collective-permute-start(f32[64,128]{1,0:T(8,128)S(1)} %get-tuple-element.65), channel_id=1, source_target_pairs={{248,0},{252,4},{0,8},{4,12},{8,16},{12,20},{16,24},{20,28},{24,32... | collective-permute-start | bytes 98312 | tf_op jit(solution)/shard_map/ppermute | solution.py:20
  255.1 11.3 %collective-permute-start.4 = (f32[64,128]{1,0:T(8,128)S(1)}, f32[64,128]{1,0:T(8,128)S(1)}, u32[]{:S(2)}, u32[]{:S(2)}) collective-permute-start(f32[64,128]{1,0:T(8,128)S(1)} %get-tuple-element.63), channel_id=1, source_target_pairs={{252,0},{0,4},{4,8},{8,12},{12,16},{16,20},{20,24},{24,28},{28,32}... | collective-permute-start | bytes 98312 | tf_op jit(solution)/shard_map/ppermute | solution.py:20
  255.8 10.6 %collective-permute-start.5 = (f32[64,128]{1,0:T(8,128)S(1)}, f32[64,128]{1,0:T(8,128)S(1)}, u32[]{:S(2)}, u32[]{:S(2)}) collective-permute-start(f32[64,128]{1,0:T(8,128)S(1)} %get-tuple-element.62), channel_id=1, source_target_pairs={{4,0},{8,4},{12,8},{16,12},{20,16},{24,20},{28,24},{32,28},{36,32}... | collective-permute-start | bytes 98312 | tf_op jit(solution)/shard_map/ppermute | solution.py:20
  260.8 7.2 %collective-permute-start.6 = (f32[64,128]{1,0:T(8,128)S(1)}, f32[64,128]{1,0:T(8,128)S(1)}, u32[]{:S(2)}, u32[]{:S(2)}) collective-permute-start(f32[64,128]{1,0:T(8,128)S(1)} %get-tuple-element.61), channel_id=1, source_target_pairs={{248,0},{252,4},{0,8},{4,12},{8,16},{12,20},{16,24},{20,28},{24,32... | collective-permute-start | bytes 98312 | tf_op jit(solution)/shard_map/ppermute | solution.py:20
  260.8 7.2 %collective-permute-start.7 = (f32[64,128]{1,0:T(8,128)S(1)}, f32[64,128]{1,0:T(8,128)S(1)}, u32[]{:S(2)}, u32[]{:S(2)}) collective-permute-start(f32[64,128]{1,0:T(8,128)S(1)} %get-tuple-element.60), channel_id=1, source_target_pairs={{8,0},{12,4},{16,8},{20,12},{24,16},{28,20},{32,24},{36,28},{40,32... | collective-permute-start | bytes 98312 | tf_op jit(solution)/shard_map/ppermute | solution.py:20
  281.5 13.0 %collective-permute-start.8 = (f32[64,128]{1,0:T(8,128)S(1)}, f32[64,128]{1,0:T(8,128)S(1)}, u32[]{:S(2)}, u32[]{:S(2)}) collective-permute-start(f32[64,128]{1,0:T(8,128)S(1)} %get-tuple-element.59), channel_id=1, source_target_pairs={{252,0},{0,4},{4,8},{8,12},{12,16},{16,20},{20,24},{24,28},{28,32}... | collective-permute-start | bytes 98312 | tf_op jit(solution)/shard_map/ppermute | solution.py:20
  283.9 10.6 %collective-permute-start.9 = (f32[64,128]{1,0:T(8,128)S(1)}, f32[64,128]{1,0:T(8,128)S(1)}, u32[]{:S(2)}, u32[]{:S(2)}) collective-permute-start(f32[64,128]{1,0:T(8,128)S(1)} %get-tuple-element.58), channel_id=1, source_target_pairs={{4,0},{8,4},{12,8},{16,12},{20,16},{24,20},{28,24},{32,28},{36,32}... | collective-permute-start | bytes 98312 | tf_op jit(solution)/shard_map/ppermute | solution.py:20
  289.0 7.2 %collective-permute-start.10 = (f32[64,128]{1,0:T(8,128)S(1)}, f32[64,128]{1,0:T(8,128)S(1)}, u32[]{:S(2)}, u32[]{:S(2)}) collective-permute-start(f32[64,128]{1,0:T(8,128)S(1)} %get-tuple-element.57), channel_id=1, source_target_pairs={{248,0},{252,4},{0,8},{4,12},{8,16},{12,20},{16,24},{20,28},{24,32... | collective-permute-start | bytes 98312 | tf_op jit(solution)/shard_map/ppermute | solution.py:20
  289.0 7.2 %collective-permute-start.11 = (f32[64,128]{1,0:T(8,128)S(1)}, f32[64,128]{1,0:T(8,128)S(1)}, u32[]{:S(2)}, u32[]{:S(2)}) collective-permute-start(f32[64,128]{1,0:T(8,128)S(1)} %get-tuple-element.56), channel_id=1, source_target_pairs={{8,0},{12,4},{16,8},{20,12},{24,16},{28,20},{32,24},{36,28},{40,32... | collective-permute-start | bytes 98312 | tf_op jit(solution)/shard_map/ppermute | solution.py:20
  307.4 17.6 %collective-permute-start.12 = (f32[64,128]{1,0:T(8,128)S(1)}, f32[64,128]{1,0:T(8,128)S(1)}, u32[]{:S(2)}, u32[]{:S(2)}) collective-permute-start(f32[64,128]{1,0:T(8,128)S(1)} %get-tuple-element.55), channel_id=1, source_target_pairs={{252,0},{0,4},{4,8},{8,12},{12,16},{16,20},{20,24},{24,28},{28,32}... | collective-permute-start | bytes 98312 | tf_op jit(solution)/shard_map/ppermute | solution.py:20
  314.2 10.9 %collective-permute-start.13 = (f32[64,128]{1,0:T(8,128)S(1)}, f32[64,128]{1,0:T(8,128)S(1)}, u32[]{:S(2)}, u32[]{:S(2)}) collective-permute-start(f32[64,128]{1,0:T(8,128)S(1)} %get-tuple-element.54), channel_id=1, source_target_pairs={{4,0},{8,4},{12,8},{16,12},{20,16},{24,20},{28,24},{32,28},{36,32}... | collective-permute-start | bytes 98312 | tf_op jit(solution)/shard_map/ppermute | solution.py:20
  319.3 7.2 %collective-permute-start.14 = (f32[64,128]{1,0:T(8,128)S(1)}, f32[64,128]{1,0:T(8,128)S(1)}, u32[]{:S(2)}, u32[]{:S(2)}) collective-permute-start(f32[64,128]{1,0:T(8,128)S(1)} %get-tuple-element.53), channel_id=1, source_target_pairs={{248,0},{252,4},{0,8},{4,12},{8,16},{12,20},{16,24},{20,28},{24,32... | collective-permute-start | bytes 98312 | tf_op jit(solution)/shard_map/ppermute | solution.py:20
  319.3 7.3 %collective-permute-start.15 = (f32[64,128]{1,0:T(8,128)S(1)}, f32[64,128]{1,0:T(8,128)S(1)}, u32[]{:S(2)}, u32[]{:S(2)}) collective-permute-start(f32[64,128]{1,0:T(8,128)S(1)} %get-tuple-element.52), channel_id=1, source_target_pairs={{8,0},{12,4},{16,8},{20,12},{24,16},{28,20},{32,24},{36,28},{40,32... | collective-permute-start | bytes 98312 | tf_op jit(solution)/shard_map/ppermute | solution.py:20
  338.5 11.0 %collective-permute-start.16 = (f32[64,128]{1,0:T(8,128)S(1)}, f32[64,128]{1,0:T(8,128)S(1)}, u32[]{:S(2)}, u32[]{:S(2)}) collective-permute-start(f32[64,128]{1,0:T(8,128)S(1)} %get-tuple-element.51), channel_id=1, source_target_pairs={{252,0},{0,4},{4,8},{8,12},{12,16},{16,20},{20,24},{24,28},{28,32}... | collective-permute-start | bytes 98312 | tf_op jit(solution)/shard_map/ppermute | solution.py:20
  338.8 11.2 %collective-permute-start.17 = (f32[64,128]{1,0:T(8,128)S(1)}, f32[64,128]{1,0:T(8,128)S(1)}, u32[]{:S(2)}, u32[]{:S(2)}) collective-permute-start(f32[64,128]{1,0:T(8,128)S(1)} %get-tuple-element.50), channel_id=1, source_target_pairs={{4,0},{8,4},{12,8},{16,12},{20,16},{24,20},{28,24},{32,28},{36,32}... | collective-permute-start | bytes 98312 | tf_op jit(solution)/shard_map/ppermute | solution.py:20
  344.0 7.2 %collective-permute-start.18 = (f32[64,128]{1,0:T(8,128)S(1)}, f32[64,128]{1,0:T(8,128)S(1)}, u32[]{:S(2)}, u32[]{:S(2)}) collective-permute-start(f32[64,128]{1,0:T(8,128)S(1)} %get-tuple-element.49), channel_id=1, source_target_pairs={{248,0},{252,4},{0,8},{4,12},{8,16},{12,20},{16,24},{20,28},{24,32... | collective-permute-start | bytes 98312 | tf_op jit(solution)/shard_map/ppermute | solution.py:20
  344.0 7.9 %collective-permute-start.19 = (f32[64,128]{1,0:T(8,128)S(1)}, f32[64,128]{1,0:T(8,128)S(1)}, u32[]{:S(2)}, u32[]{:S(2)}) collective-permute-start(f32[64,128]{1,0:T(8,128)S(1)} %get-tuple-element.48), channel_id=1, source_target_pairs={{8,0},{12,4},{16,8},{20,12},{24,16},{28,20},{32,24},{36,28},{40,32... | collective-permute-start | bytes 98312 | tf_op jit(solution)/shard_map/ppermute | solution.py:20
  366.8 11.4 %collective-permute-start.20 = (f32[64,128]{1,0:T(8,128)S(1)}, f32[64,128]{1,0:T(8,128)S(1)}, u32[]{:S(2)}, u32[]{:S(2)}) collective-permute-start(f32[64,128]{1,0:T(8,128)S(1)} %get-tuple-element.47), channel_id=1, source_target_pairs={{252,0},{0,4},{4,8},{8,12},{12,16},{16,20},{20,24},{24,28},{28,32}... | collective-permute-start | bytes 98312 | tf_op jit(solution)/shard_map/ppermute | solution.py:20
  367.8 10.4 %collective-permute-start.21 = (f32[64,128]{1,0:T(8,128)S(1)}, f32[64,128]{1,0:T(8,128)S(1)}, u32[]{:S(2)}, u32[]{:S(2)}) collective-permute-start(f32[64,128]{1,0:T(8,128)S(1)} %get-tuple-element.46), channel_id=1, source_target_pairs={{4,0},{8,4},{12,8},{16,12},{20,16},{24,20},{28,24},{32,28},{36,32}... | collective-permute-start | bytes 98312 | tf_op jit(solution)/shard_map/ppermute | solution.py:20
  372.9 7.2 %collective-permute-start.22 = (f32[64,128]{1,0:T(8,128)S(1)}, f32[64,128]{1,0:T(8,128)S(1)}, u32[]{:S(2)}, u32[]{:S(2)}) collective-permute-start(f32[64,128]{1,0:T(8,128)S(1)} %get-tuple-element.45), channel_id=1, source_target_pairs={{248,0},{252,4},{0,8},{4,12},{8,16},{12,20},{16,24},{20,28},{24,32... | collective-permute-start | bytes 98312 | tf_op jit(solution)/shard_map/ppermute | solution.py:20
  372.9 7.2 %collective-permute-start.23 = (f32[64,128]{1,0:T(8,128)S(1)}, f32[64,128]{1,0:T(8,128)S(1)}, u32[]{:S(2)}, u32[]{:S(2)}) collective-permute-start(f32[64,128]{1,0:T(8,128)S(1)} %get-tuple-element.44), channel_id=1, source_target_pairs={{8,0},{12,4},{16,8},{20,12},{24,16},{28,20},{32,24},{36,28},{40,32... | collective-permute-start | bytes 98312 | tf_op jit(solution)/shard_map/ppermute | solution.py:20
  389.0 12.0 %collective-permute-start.24 = (f32[64,128]{1,0:T(8,128)S(1)}, f32[64,128]{1,0:T(8,128)S(1)}, u32[]{:S(2)}, u32[]{:S(2)}) collective-permute-start(f32[64,128]{1,0:T(8,128)S(1)} %get-tuple-element.43), channel_id=1, source_target_pairs={{252,0},{0,4},{4,8},{8,12},{12,16},{16,20},{20,24},{24,28},{28,32}... | collective-permute-start | bytes 98312 | tf_op jit(solution)/shard_map/ppermute | solution.py:20
  390.4 10.7 %collective-permute-start.25 = (f32[64,128]{1,0:T(8,128)S(1)}, f32[64,128]{1,0:T(8,128)S(1)}, u32[]{:S(2)}, u32[]{:S(2)}) collective-permute-start(f32[64,128]{1,0:T(8,128)S(1)} %get-tuple-element.42), channel_id=1, source_target_pairs={{4,0},{8,4},{12,8},{16,12},{20,16},{24,20},{28,24},{32,28},{36,32}... | collective-permute-start | bytes 98312 | tf_op jit(solution)/shard_map/ppermute | solution.py:20
  395.7 7.2 %collective-permute-start.26 = (f32[64,128]{1,0:T(8,128)S(1)}, f32[64,128]{1,0:T(8,128)S(1)}, u32[]{:S(2)}, u32[]{:S(2)}) collective-permute-start(f32[64,128]{1,0:T(8,128)S(1)} %get-tuple-element.41), channel_id=1, source_target_pairs={{248,0},{252,4},{0,8},{4,12},{8,16},{12,20},{16,24},{20,28},{24,32... | collective-permute-start | bytes 98312 | tf_op jit(solution)/shard_map/ppermute | solution.py:20
  395.7 7.2 %collective-permute-start.27 = (f32[64,128]{1,0:T(8,128)S(1)}, f32[64,128]{1,0:T(8,128)S(1)}, u32[]{:S(2)}, u32[]{:S(2)}) collective-permute-start(f32[64,128]{1,0:T(8,128)S(1)} %get-tuple-element.40), channel_id=1, source_target_pairs={{8,0},{12,4},{16,8},{20,12},{24,16},{28,20},{32,24},{36,28},{40,32... | collective-permute-start | bytes 98312 | tf_op jit(solution)/shard_map/ppermute | solution.py:20
  411.8 173.4 %collective-permute-start.28 = (f32[64,128]{1,0:T(8,128)S(1)}, f32[64,128]{1,0:T(8,128)S(1)}, u32[]{:S(2)}, u32[]{:S(2)}) collective-permute-start(f32[64,128]{1,0:T(8,128)S(1)} %get-tuple-element.39), channel_id=1, source_target_pairs={{252,0},{0,4},{4,8},{8,12},{12,16},{16,20},{20,24},{24,28},{28,32}... | collective-permute-start | bytes 98312 | tf_op jit(solution)/shard_map/ppermute | solution.py:20
  576.6 8.7 %collective-permute-start.29 = (f32[64,128]{1,0:T(8,128)S(1)}, f32[64,128]{1,0:T(8,128)S(1)}, u32[]{:S(2)}, u32[]{:S(2)}) collective-permute-start(f32[64,128]{1,0:T(8,128)S(1)} %get-tuple-element.38), channel_id=1, source_target_pairs={{4,0},{8,4},{12,8},{16,12},{20,16},{24,20},{28,24},{32,28},{36,32}... | collective-permute-start | bytes 98312 | tf_op jit(solution)/shard_map/ppermute | solution.py:20
  579.9 7.2 %collective-permute-start.30 = (f32[64,128]{1,0:T(8,128)S(1)}, f32[64,128]{1,0:T(8,128)S(1)}, u32[]{:S(2)}, u32[]{:S(2)}) collective-permute-start(f32[64,128]{1,0:T(8,128)S(1)} %get-tuple-element.37), channel_id=1, source_target_pairs={{248,0},{252,4},{0,8},{4,12},{8,16},{12,20},{16,24},{20,28},{24,32... | collective-permute-start | bytes 98312 | tf_op jit(solution)/shard_map/ppermute | solution.py:20
  579.9 7.2 %collective-permute-start.31 = (f32[64,128]{1,0:T(8,128)S(1)}, f32[64,128]{1,0:T(8,128)S(1)}, u32[]{:S(2)}, u32[]{:S(2)}) collective-permute-start(f32[64,128]{1,0:T(8,128)S(1)} %get-tuple-element.36), channel_id=1, source_target_pairs={{8,0},{12,4},{16,8},{20,12},{24,16},{28,20},{32,24},{36,28},{40,32... | collective-permute-start | bytes 98312 | tf_op jit(solution)/shard_map/ppermute | solution.py:20
  (17 other events, 163.1 us)
Sparse Core Ops, SparseCore 0:
  390.5 184.1 all-reduce.1
